TPU v7x, 256 devices: a whole 4x4x8 slice. The times are simulated.
256 devices in a mesh: shard: 64 (over z, y, core), help: 4 (over x).
Axes of the slice: x: 4, y: 4, z: 8, core: 2. Of those that a mesh axis runs over, the one named last changes fastest.
Arguments:
- queries: bfloat16 [65536, 768], P(('shard', 'help')), may hold values from -6 to 6
- probe_group: int32 [65536, 2], P(('shard', 'help')), may hold values from 0 to 63, all different within a row; in each aligned block of 256 rows (0 to 255, 256 to 511, ...) at most 16 rows name the same one
- probe_local: int32 [65536, 2], P(('shard', 'help')), may hold values from 0 to 3
- points: bfloat16 [262144, 768], P(('shard', 'help')), may hold values from -6 to 6
- point_cluster: int32 [64, 4096], P('shard'), may hold values from 0 to 3, never falling along the last dimension, each value on 1 to 3072 neighbouring positions
- test_matrix: bfloat16 [32, 262144], P(None, ('shard', 'help')), may hold values from -6 to 6
Outputs:
- sketch: float32 [32, 262144], P(None, ('shard', 'help'))
- regressor: float32 [256, 32, 768], P(('shard', 'help'))
Inputs may be any that keep to these rules, and one draw needn't show every extreme that they name: `probe_group`: A query's 2 groups differ. Among the 256 queries of one device (aligned blocks of rows), at most 16 pairs (q,k) name one group, and in some blocks one group is named exactly 16 times.
All inputs are finite; a program needn't handle non-finite values.
Results may differ from a plain program's by a relative error of at most 0.0037.
Values may be sent and summed in bfloat16 or wider, within the bound.
A program may use at most 64 MiB of HBM per device.

v0:
```python
import jax
import jax.numpy as jnp
from jax import lax
from jax.sharding import PartitionSpec as P

PROBES = 2
CL_DEV = 1


def masked_scores(point_rows, point_ids, query_rows, query_ids):
    feature_width = point_rows.shape[1]
    block_rows = min(512, point_rows.shape[0])
    factor = feature_width ** (-0.5)

    def score_piece(pieces):
        piece_x, piece_ids = pieces
        product = (
            lax.dot_general(
                piece_x, query_rows, (((1,), (1,)), ((), ())), preferred_element_type=jnp.float32
            )
            * factor
        )
        return jnp.where(piece_ids[:, None] == query_ids[None, :], product, 0.0).astype(
            jnp.bfloat16
        )

    stacked = lax.map(
        score_piece,
        (point_rows.reshape(-1, block_rows, feature_width), point_ids.reshape(-1, block_rows)),
    )
    return stacked.reshape(point_rows.shape[0], query_rows.shape[0])


def pack_rows(source, target, member, groups, blocks, capacity, probes):
    feature_width = source.shape[1]
    row_total = target.shape[0]
    per_block = row_total // blocks
    labels = jnp.arange(groups, dtype=jnp.int32)
    onehot_dest = (
        (target[:, None] == labels[None, :]).astype(jnp.int32).reshape(blocks, per_block, groups)
    )
    ranking = jnp.sum((jnp.cumsum(onehot_dest, axis=1) - onehot_dest) * onehot_dest, axis=2)
    position = (
        target.reshape(blocks, per_block) * (blocks * capacity)
        + jnp.arange(blocks, dtype=jnp.int32)[:, None] * capacity
        + ranking
    )
    position = position.reshape(-1)
    copied_rows = jnp.repeat(source, probes, axis=0)
    filled = (
        jnp.zeros((groups * blocks * capacity, feature_width), jnp.bfloat16)
        .at[position]
        .set(copied_rows)
    )
    labelled = jnp.full((groups * blocks * capacity,), -1, jnp.int32).at[position].set(member)
    return (
        filled.reshape(groups, blocks * capacity, feature_width),
        labelled.reshape(groups, blocks * capacity),
    )


def count_labels(ids, labels):
    return jnp.sum((ids[None, :] == labels[:, None]).astype(jnp.float32), axis=1)


def shards(queries, probe_group, probe_local, points, point_cluster, test_matrix):
    groups = lax.axis_size("shard")
    helpers = lax.axis_size("help")
    helper = lax.axis_index("help")
    feature_width = queries.shape[1]
    per_device = queries.shape[0] * PROBES
    capacity = 2 * per_device // groups
    group_clusters = CL_DEV * helpers
    own_points = points.shape[0]
    group_ids = point_cluster[0]
    own_ids = lax.dynamic_slice_in_dim(group_ids, helper * own_points, own_points, 0)
    labels = jnp.arange(group_clusters, dtype=jnp.int32)
    resident = count_labels(group_ids, labels)
    peer_rows, peer_groups, peer_local = (
        lax.all_gather(queries, "help", axis=0, tiled=True),
        lax.all_gather(probe_group, "help", axis=0, tiled=True),
        lax.all_gather(probe_local, "help", axis=0, tiled=True),
    )
    outgoing, out_ids = pack_rows(
        peer_rows,
        peer_groups.reshape(-1),
        peer_local.reshape(-1),
        groups,
        helpers,
        capacity,
        PROBES,
    )
    query_pool, pool_ids = (
        lax.all_to_all(outgoing, "shard", split_axis=0, concat_axis=0, tiled=True),
        lax.all_to_all(out_ids, "shard", split_axis=0, concat_axis=0, tiled=True),
    )
    query_rows = query_pool.reshape(-1, feature_width)
    query_ids = pool_ids.reshape(-1)
    scores = masked_scores(points, own_ids, query_rows, query_ids)
    lifted = lax.psum(
        jnp.dot(test_matrix, scores, preferred_element_type=jnp.float32), "help"
    ).astype(jnp.bfloat16)
    product = lax.dot_general(
        lifted, scores, (((1,), (1,)), ((), ())), preferred_element_type=jnp.float32
    )
    queried = count_labels(query_ids, labels)
    factor = 1.0 / jnp.sqrt((queried + 1.0) * (queried + resident))
    own_hot = (own_ids[None, :] == labels[:, None]).astype(jnp.float32)
    sketch = product * jnp.sum(factor[:, None] * own_hot, axis=0)[None, :]
    rounded = sketch.astype(jnp.bfloat16)
    hot_rows = own_hot.astype(jnp.bfloat16)
    weighted = (hot_rows[:, None, :] * rounded[None, :, :]).reshape(
        CL_DEV * lax.axis_size("help") * rounded.shape[0], own_points
    )
    summed = jnp.dot(weighted, points, preferred_element_type=jnp.float32)
    partial_sum = lax.psum_scatter(
        summed.reshape(CL_DEV * lax.axis_size("help"), rounded.shape[0], feature_width),
        "help",
        scatter_dimension=0,
        tiled=True,
    )
    scale_own = lax.dynamic_slice_in_dim(1.0 / jnp.sqrt(resident), helper * CL_DEV, CL_DEV, 0)
    regressor = partial_sum * scale_own[:, None, None]
    return (sketch, regressor)


def solution(mesh):
    in_specs = (
        P(("shard", "help"), None),
        P(("shard", "help"), None),
        P(("shard", "help"), None),
        P(("shard", "help"), None),
        P("shard", None),
        P(None, ("shard", "help")),
    )
    out_specs = (P(None, ("shard", "help")), P(("shard", "help"), None, None))
    return jax.shard_map(shards, mesh=mesh, in_specs=in_specs, out_specs=out_specs, check_vma=False)
```

profile of v0, /device:TPU:32, one launch (start us, length us, event | category | flops | bytes accessed | tf_op | source)
XLA Modules:
  0.0 306.9 jit_solution(3238835004986476215)
XLA Ops:
  7.2 0.7 all-gather.2.cloned.1.call-update
  7.9 11.3 %all_gather.9 = s32[1024,2]{0,1:T(2,128)S(1)} all-gather(s32[256,2]{0,1:T(2,128)} %param.9), channel_id=1, replica_groups=mesh['shard'=64,'help'=4] {'help'}, dimensions={0}, use_global_device_ids=true | all-gather | bytes 10240 | tf_op jit(solution)/shard_map/all_gather | solution.py:81
  19.2 0.2 copy.19
  19.4 0.3 eq.96
  19.7 0.3 eq.92
  20.1 4.8 %reduce-window.6 = s32[4,64,4,128]{3,1,2,0:T(8,128)S(1)} reduce-window(s32[4,64,4,128]{3,1,2,0:T(8,128)S(1)} %fusion.12, s32[]{:T(128)} %constant.9.clone.1), window={size=1x1x1x128 pad=0_0x0_0x0_0x127_0}, to_apply=%region_0.0 | reduce-window | flops 16646144 | bytes 1048580 | tf_op jit(solution)/shard_map/reduce-window
  24.9 0.5 slice_reduce_fusion
  25.5 0.2 fusion.11
  25.9 0.3 mul.85
  26.4 10.8 %all_gather.10 = s32[1024,2]{0,1:T(2,128)S(1)} all-gather(s32[256,2]{0,1:T(2,128)} %param.10), channel_id=1, replica_groups=mesh['shard'=64,'help'=4] {'help'}, dimensions={0}, use_global_device_ids=true | all-gather | bytes 10240 | tf_op jit(solution)/shard_map/all_gather | solution.py:82
  37.4 0.3 reshape.158
  37.7 8.1 %scatter_custom_fusion = s32[4096]{0:T(1024)S(1)} fusion(s32[2048]{0:T(1024)S(1)} %bitcast.81, s32[2048]{0:T(1024)S(1)} %reshape.158, s32[]{:T(128)} %constant.20.clone.1), kind=kCustom, calls=%fused_computation.37 | custom fusion | bytes 16388 | tf_op jit(solution)/shard_map/scatter | solution.py:55
  45.7 0.7 all_to_all.11
  46.4 11.8 %all-to-all-start = ((s32[64,1,64]{2,1,0:T(1,128)}), s32[64,1,64]{2,1,0:T(1,128)S(1)}, u32[]{:S(2)}, u32[]{:S(2)}) async-start(s32[64,1,64]{2,1,0:T(1,128)} %all_to_all.11), calls=%async_computation | async-start | bytes 65536 | tf_op jit(solution)/shard_map/all_to_all | solution.py:95
  58.2 3.0 broadcast_in_dim.20
  61.3 2.7 reshape.166
  64.0 13.9 %scatter_custom_fusion.1 = bf16[4096,768]{1,0:T(8,128)(2,1)} fusion(s32[2048]{0:T(1024)S(1)} %bitcast.82, bf16[2048,768]{1,0:T(8,128)(2,1)} %reshape.166, bf16[]{:T(256)} %constant.22.clone.1), kind=kCustom, calls=%fused_computation.10 | custom fusion | bytes 6291968 | tf_op jit(solution)/shard_map/scatter | solution.py:53
  77.9 10.6 %all-to-all-start.1 = ((bf16[64,64,768]{2,1,0:T(8,128)(2,1)}), bf16[64,64,768]{2,1,0:T(8,128)(2,1)}, u32[]{:S(2)}, u32[]{:S(2)}) async-start(bf16[64,64,768]{2,1,0:T(8,128)(2,1)} %bitcast.69), calls=%async_computation.1 | async-start | bytes 12582912 | tf_op jit(solution)/shard_map/all_to_all | solution.py:94
  88.6 0.5 broadcast.103
  89.1 0.7 fusion.19
  89.9 0.7 reduce.9
  91.0 138.0 %all-to-all-done.1 = bf16[64,64,768]{2,1,0:T(8,128)(2,1)} async-done(((bf16[64,64,768]{2,1,0:T(8,128)(2,1)}), bf16[64,64,768]{2,1,0:T(8,128)(2,1)}, u32[]{:S(2)}, u32[]{:S(2)}) %all-to-all-start.1) | async-done | bytes 6291488 | tf_op jit(solution)/shard_map/all_to_all | solution.py:94
  229.0 15.6 %while.11 = (s32[]{:T(128)}, bf16[2,512,4096]{2,1,0:T(8,128)(2,1)}, s32[2,512]{1,0:T(2,128)S(1)}, s32[64,64]{1,0:T(8,128)}, bf16[2,512,768]{2,1,0:T(8,128)(2,1)S...) while((s32[]{:T(128)}, bf16[2,512,4096]{2,1,0:T(8,128)(2,1)}, ...), condition=%wide.wide.region_6.7_spmd, body=%wide.wide.region_5.6_spmd.sunk | while | flops 3229614080 | bytes 11295833 | solution.py:27
  229.0 7.8 %fusion.35 = bf16[2,512,4096]{2,1,0:T(8,128)(2,1)} fusion(bf16[2,512,4096]{2,1,0:T(8,128)(2,1)} %get-tuple-element.131, s32[]{:T(128)} %get-tuple-element.130, bf16[4096,768]{1,0:T(8,128)(2,1)} %get-tuple-element.143, s32[4096]{0:T(1024)S(1)} %get-tuple-element.144, s32[512]{0:T(512)S(1)} %bitcast.74, ...), kind=kOutput, calls=%fused_computation.4.clone.clone.1 | convolution fusion | flops 3229614080 | bytes 11291648 | tf_op jit(solution)/shard_map/while/body/eval_jaxpr/dot_general | solution.py:18
  236.8 7.8 %fusion.35 = bf16[2,512,4096]{2,1,0:T(8,128)(2,1)} fusion(bf16[2,512,4096]{2,1,0:T(8,128)(2,1)} %get-tuple-element.131, s32[]{:T(128)} %get-tuple-element.130, bf16[4096,768]{1,0:T(8,128)(2,1)} %get-tuple-element.143, s32[4096]{0:T(1024)S(1)} %get-tuple-element.144, s32[512]{0:T(512)S(1)} %bitcast.74, ...), kind=kOutput, calls=%fused_computation.4.clone.clone.1 | convolution fusion | flops 3229614080 | bytes 11291648 | tf_op jit(solution)/shard_map/while/body/eval_jaxpr/dot_general | solution.py:18
  244.6 4.9 %convolution_bitcast_fusion = f32[32,4096]{1,0:T(8,128)S(1)} fusion(bf16[32,1024]{1,0:T(8,128)(2,1)S(1)} %copy-done, bf16[1024,4096]{1,0:T(8,128)(2,1)} %bitcast.67), kind=kOutput, calls=%fused_computation.9 | convolution fusion | flops 268435456 | bytes 8978432 | tf_op jit(solution)/shard_map/dot_general | solution.py:101
  249.5 21.5 %all-reduce.1 = bf16[32,4096]{1,0:T(8,128)(2,1)S(1)} all-reduce(f32[32,4096]{1,0:T(8,128)S(1)} %convolution_bitcast_fusion), channel_id=1, replica_groups=mesh['shard'=64,'help'=4] {'help'}, use_global_device_ids=true, to_apply=%region_7.8 | all-reduce | flops 131072 | bytes 786432 | tf_op jit(solution)/shard_map/psum | solution.py:100
  271.0 6.6 %fusion.21 = (bf16[32,1024]{1,0:T(8,128)(2,1)S(1)}, f32[32,1024]{1,0:T(8,128)}) fusion(f32[1024]{0:T(1024)S(1)} %select_reduce_fusion, bf16[32,4096]{1,0:T(8,128)(2,1)S(1)} %all-reduce.1, bf16[1024,4096]{1,0:T(8,128)(2,1)} %bitcast.68), kind=kOutput, calls=%fused_computation.46 | convolution fusion | flops 268500992 | bytes 8851456 | tf_op jit(solution)/shard_map/dot_general | solution.py:103
  277.6 1.1 fusion.7
  278.7 0.6 dynamic_slice.15
  279.4 18.5 %reduce-scatter.2.cloned.1.call-done = f32[1,32,768]{2,1,0:T(8,128)} async-done(((f32[4,32,768]{2,1,0:T(8,128)}), f32[1,32,768]{2,1,0:T(8,128)}) %reduce-scatter.2.cloned.1.call-update) | async-done | bytes 98320 | tf_op jit(solution)/shard_map/reduce_scatter | solution.py:116
  297.9 2.2 broadcast_multiply_fusion
  (34 shorter events, 1.2 us)
Async XLA Ops:
  7.2 237.4 %copy-start = (bf16[32,1024]{1,0:T(8,128)(2,1)S(1)}, bf16[32,1024]{1,0:T(8,128)(2,1)}, u32[]{:S(2)}) copy-start(bf16[32,1024]{1,0:T(8,128)(2,1)} %param.13) | copy-start | bytes 196612
  7.2 51.0 %all-gather.2.cloned.1.call-start = ((), (), s32[]{:S(2)}) async-start(), calls=%async_computation.3 | async-start | bytes 1966080 | tf_op jit(solution)/shard_map/all_gather | solution.py:80
  46.4 31.4 %all-to-all-start = ((s32[64,1,64]{2,1,0:T(1,128)}), s32[64,1,64]{2,1,0:T(1,128)S(1)}, u32[]{:S(2)}, u32[]{:S(2)}) async-start(s32[64,1,64]{2,1,0:T(1,128)} %all_to_all.11), calls=%async_computation | async-start | bytes 65536 | tf_op jit(solution)/shard_map/all_to_all | solution.py:95
  77.9 12.0 %copy-start.2 = (s32[64,1,64]{2,1,0:T(1,128)}, s32[64,1,64]{2,1,0:T(1,128)S(1)}, u32[]{:S(2)}) copy-start(s32[64,1,64]{2,1,0:T(1,128)S(1)} %all-to-all-done) | copy-start | bytes 49156
  77.9 11.2 %copy-start.3 = (s32[1,4096]{1,0:T(1,128)S(1)}, s32[1,4096]{1,0:T(1,128)}, u32[]{:S(2)}) copy-start(s32[1,4096]{1,0:T(1,128)} %param.12) | copy-start | bytes 49156
  77.9 151.1 %copy-start.1 = (bf16[1024,768]{1,0:T(8,128)(2,1)S(1)}, bf16[1024,768]{1,0:T(8,128)(2,1)}, u32[]{:S(2)}) copy-start(bf16[1024,768]{1,0:T(8,128)(2,1)} %param.11) | copy-start | bytes 4718596
  77.9 151.1 %all-to-all-start.1 = ((bf16[64,64,768]{2,1,0:T(8,128)(2,1)}), bf16[64,64,768]{2,1,0:T(8,128)(2,1)}, u32[]{:S(2)}, u32[]{:S(2)}) async-start(bf16[64,64,768]{2,1,0:T(8,128)(2,1)} %bitcast.69), calls=%async_computation.1 | async-start | bytes 12582912 | tf_op jit(solution)/shard_map/all_to_all | solution.py:94
  88.5 209.4 %reduce-scatter.2.cloned.1.call-start = ((), (), s32[]{:S(2)}) async-start(), calls=%async_computation.4 | async-start | bytes 491520 | tf_op jit(solution)/shard_map/reduce_scatter | solution.py:116
Sparse Core Ops, SparseCore 0:
  9.8 31.6 all-gather.1
  278.9 18.9 reduce-scatter.1
where the time goes:
time: 308 us; the launch traced here: 307 us
  waiting for transfers between devices  157 us (51%)
  blocking collectives  43.5 us (14%)
  local copies, waits for them, and re-layouts  32.8 us (11%)
  matrix products  28.3 us (9%)
  starting transfers between devices  22.4 us (7%)
  between operations  14.2 us (5%)
  other arithmetic  8.3 us (3%)
    all_to_all x1, waiting for transfers between devices, shards(): lax.all_to_all(outgoing, 'shard', split_axis=0, concat_axis=0, tiled=True)  138 us
    psum x1, blocking collectives, shards(): lax.psum(jnp.dot(test_matrix, scores, preferred_element_type=jnp.float32)...  21.5 us
    reduce_scatter x1, waiting for transfers between devices, shards(): lax.psum_scatter(summed.reshape(CL_DEV * lax.axis_size('help'), rounded.s...  18.5 us
    dot_general x2, matrix products, score_piece(): lax.dot_general(piece_x, query_rows, (((1,), (1,)), ((), ())), preferred_...  15.6 us
    scatter x1, local copies, waits for them, and re-layouts, pack_rows(): filled = jnp.zeros((groups * blocks * capacity, feature_width), jnp.bfloa...  13.9 us
    all_to_all x1, starting transfers between devices, shards(): lax.all_to_all(out_ids, 'shard', split_axis=0, concat_axis=0, tiled=True)  11.8 us
    all_gather x1, blocking collectives, shards(): lax.all_gather(probe_group, 'help', axis=0, tiled=True)  11.3 us
    all_gather x1, blocking collectives, shards(): lax.all_gather(probe_local, 'help', axis=0, tiled=True)  10.8 us
  transfers between devices with their start and end apart: 4, of which 2 were waited for; matrix products, arithmetic and copies ran while one was open for 12% of the time, Pallas kernels for 0%

commit v1 on v0

v1 whole, which is shorter than its diff:
```python
import jax
import jax.numpy as jnp
from jax import lax
from jax.sharding import PartitionSpec as P

F32 = jnp.float32
BF16 = jnp.bfloat16


def split(v):
    hi = v.astype(BF16)
    lo = (v - hi.astype(F32)).astype(BF16)
    return hi, lo


def dot2(v, w, dims):
    hi, lo = split(v)
    return lax.dot_general(hi, w, (dims, ((), ())), preferred_element_type=F32) + lax.dot_general(
        lo, w, (dims, ((), ())), preferred_element_type=F32
    )


def shards(queries, probe_group, probe_local, points, point_cluster, test_matrix):
    groups = lax.axis_size("shard")
    helpers = lax.axis_size("help")
    helper = lax.axis_index("help")
    rows, width = queries.shape
    probes = probe_group.shape[1]
    capacity = 2 * rows * probes // groups
    slots = groups * capacity
    rank = test_matrix.shape[0]
    own_points = points.shape[0]
    clusters = helpers
    scale = width ** (-0.5)

    target = probe_group.reshape(-1)
    hot = (target[:, None] == jnp.arange(groups, dtype=jnp.int32)[None, :]).astype(BF16)
    pairs = rows * probes
    before = (
        jnp.arange(pairs, dtype=jnp.int32)[:, None] > jnp.arange(pairs, dtype=jnp.int32)[None, :]
    ).astype(BF16)
    counts = jnp.dot(before, hot, preferred_element_type=F32)
    place = target * capacity + jnp.sum(counts * hot.astype(F32), axis=1).astype(jnp.int32)
    place = place.reshape(rows, probes)
    slot = jnp.arange(slots, dtype=jnp.int32)
    hit = [(slot[:, None] == place[:, k][None, :]) for k in range(probes)]
    packed = jnp.dot(
        (hit[0] | hit[1]).astype(BF16), queries, preferred_element_type=F32
    ).astype(BF16)
    ids = -1 + sum(
        jnp.sum(jnp.where(hit[k], probe_local[:, k][None, :] + 1, 0), axis=1) for k in range(probes)
    )
    pool = lax.all_to_all(
        packed.reshape(groups, capacity, width), "shard", split_axis=0, concat_axis=0, tiled=True
    ).reshape(slots, width)
    pool_ids = lax.all_to_all(
        ids.astype(jnp.int32).reshape(groups, 1, capacity), "shard", split_axis=0, concat_axis=0, tiled=True
    ).reshape(slots)

    group_ids = point_cluster[0]
    own_ids = lax.dynamic_slice_in_dim(group_ids, helper * own_points, own_points, 0)
    labels = jnp.arange(clusters, dtype=jnp.int32)
    resident = jnp.sum((group_ids[None, :] == labels[:, None]).astype(F32), axis=1)
    own_hot = own_ids[None, :] == labels[:, None]

    spread = jnp.where(own_hot[:, None, :], test_matrix[None], 0).reshape(clusters * rank, own_points)
    lead = lax.psum(jnp.dot(spread, points, preferred_element_type=F32), "help")
    lifted = dot2(lead * scale, pool, ((1,), (1,)))
    pool_hot = pool_ids[None, :] == labels[:, None]
    lifted = jnp.where(pool_hot[:, None, :], lifted.reshape(clusters, rank, slots), 0.0).reshape(
        clusters * rank, slots
    )
    back = dot2(lifted * scale, pool, ((1,), (0,)))
    named = jnp.sum(pool_hot.astype(F32), axis=1)
    back, queried = lax.psum((back, named), "help")
    product = dot2(back, points, ((1,), (1,))).reshape(clusters, rank, own_points)
    factor = 1.0 / jnp.sqrt((queried + 1.0) * (queried + resident))
    sketch = jnp.sum(jnp.where(own_hot[:, None, :], product * factor[:, None, None], 0.0), axis=0)
    rounded = sketch.astype(BF16)
    weighted = jnp.where(own_hot[:, None, :], rounded[None], 0).reshape(clusters * rank, own_points)
    summed = jnp.dot(weighted, points, preferred_element_type=F32)
    own = lax.psum_scatter(
        summed.reshape(clusters, rank, width), "help", scatter_dimension=0, tiled=True
    )
    own_scale = lax.dynamic_slice_in_dim(1.0 / jnp.sqrt(resident), helper, 1, 0)
    return (sketch, own * own_scale[:, None, None])


def solution(mesh):
    in_specs = (
        P(("shard", "help"), None),
        P(("shard", "help"), None),
        P(("shard", "help"), None),
        P(("shard", "help"), None),
        P("shard", None),
        P(None, ("shard", "help")),
    )
    out_specs = (P(None, ("shard", "help")), P(("shard", "help"), None, None))
    return jax.shard_map(shards, mesh=mesh, in_specs=in_specs, out_specs=out_specs, check_vma=False)
```

time: 308 us -> 179 us (0.58)
  waiting for transfers between devices: 157 us -> 116 us
  blocking collectives: 43.5 us -> 9.33 us
  local copies, waits for them, and re-layouts: 32.8 us -> 3.95 us
  matrix products: 28.3 us -> 11.6 us
  starting transfers between devices: 22.4 us -> 17.6 us
  other arithmetic: 8.3 us -> 5.17 us
    all_to_all x2, waiting for transfers between devices: 138 us -> 5.81 us  [the longest x1 5.81 us: shards(): lax.all_to_all(ids.astype(jnp.int32).reshape(groups, 1, capacity), 'shard...]
    psum x0 -> x2, waiting for transfers between devices: none -> 86.9 us  [the longest x1 48.3 us: shards(): lead = lax.psum(jnp.dot(spread, points, preferred_element_type=F32), 'help')]
    all_gather x2 -> x0, blocking collectives: 22.1 us -> none  [the longest x1 11.3 us: shards(): lax.all_gather(probe_group, 'help', axis=0, tiled=True)]
    scatter x2 -> x0, local copies, waits for them, and re-layouts: 22 us -> none  [the longest x1 13.9 us: pack_rows(): filled = jnp.zeros((groups * blocks * capacity, feature_width), jnp.bfloa...]
    dot_general x5 -> x10, matrix products: 28.3 us -> 11.6 us  [the longest x3 3.8 us: dot2(): lax.dot_general(hi, w, (dims, ((), ())), preferred_element_type=F32)]
    psum x1, blocking collectives: 21.5 us -> 9.33 us  [shards(): back, queried = lax.psum((back, named), 'help')]
    reduce_scatter x1, waiting for transfers between devices: 18.5 us -> 23.7 us  [shards(): lax.psum_scatter(summed.reshape(clusters, rank, width), 'help', scatter_d...]
    all_to_all x2, starting transfers between devices: 22.4 us -> 17.5 us  [the longest x1 11.8 us: shards(): lax.all_to_all(ids.astype(jnp.int32).reshape(groups, 1, capacity), 'shard...]
  transfers between devices with their start and end apart: 4 -> 5, of which waited for: 2 -> 4; matrix products, arithmetic and copies ran while one was open for 12% -> 4% of each run, Pallas kernels for 0% -> 0%
where the time goes in v1:
time: 179 us; the launch traced here: 178 us
  waiting for transfers between devices  116 us (65%)
  starting transfers between devices  17.6 us (10%)
  between operations  13.9 us (8%)
  matrix products  11.6 us (6%)
  blocking collectives  9.33 us (5%)
  other arithmetic  5.17 us (3%)
  local copies, waits for them, and re-layouts  3.95 us (2%)
    psum x1, waiting for transfers between devices, shards(): lead = lax.psum(jnp.dot(spread, points, preferred_element_type=F32), 'help')  48.3 us
    psum x1, waiting for transfers between devices, shards(): back, queried = lax.psum((back, named), 'help')  38.5 us
    reduce_scatter x1, waiting for transfers between devices, shards(): lax.psum_scatter(summed.reshape(clusters, rank, width), 'help', scatter_d...  23.7 us
    all_to_all x1, starting transfers between devices, shards(): lax.all_to_all(ids.astype(jnp.int32).reshape(groups, 1, capacity), 'shard...  11.8 us
    psum x1, blocking collectives, shards(): back, queried = lax.psum((back, named), 'help')  9.33 us
    all_to_all x1, waiting for transfers between devices, shards(): lax.all_to_all(ids.astype(jnp.int32).reshape(groups, 1, capacity), 'shard...  5.81 us
    all_to_all x1, starting transfers between devices, shards(): lax.all_to_all(packed.reshape(groups, capacity, width), 'shard', split_ax...  5.72 us
    dot_general x3, matrix products, dot2(): lax.dot_general(hi, w, (dims, ((), ())), preferred_element_type=F32)  3.8 us
  transfers between devices with their start and end apart: 5, of which 4 were waited for; matrix products, arithmetic and copies ran while one was open for 4% of the time, Pallas kernels for 0%

profile of v1, /device:TPU:32, one launch (start us, length us, event | category | flops | bytes accessed | tf_op | source)
XLA Modules:
  0.0 178.0 jit_solution(8546420351986458754)
XLA Ops:
  7.2 0.9 copy.22
  8.1 0.1 eq.103
  8.3 0.3 fusion.4
  8.6 0.1 convert_element_type.64
  8.8 0.7 multiply_add_fusion
  9.5 0.8 slice_add_fusion
  10.3 0.3 select_reduce_fusion
  10.6 0.7 add.91
  11.3 11.8 %all-to-all-start = ((s32[64,1,16]{2,1,0:T(1,128)}), s32[64,1,16]{2,1,0:T(1,128)S(1)}, u32[]{:S(2)}, u32[]{:S(2)}) async-start(s32[64,1,16]{2,1,0:T(1,128)} %bitcast.5), calls=%async_computation | async-start | bytes 65536 | tf_op jit(solution)/shard_map/all_to_all | solution.py:56
  23.1 2.8 %convolution_convert_fusion = bf16[1024,768]{1,0:T(8,128)(2,1)} fusion(bf16[256,768]{1,0:T(8,128)(2,1)} %param.6, s32[256]{0:T(256)S(1)} %bitcast.38, s32[256]{0:T(256)S(1)} %bitcast.36), kind=kOutput, calls=%fused_computation | convolution fusion | flops 404226048 | bytes 1968128 | tf_op jit(solution)/shard_map/dot_general | solution.py:47
  25.8 5.8 %all-to-all-done = s32[64,1,16]{2,1,0:T(1,128)S(1)} async-done(((s32[64,1,16]{2,1,0:T(1,128)}), s32[64,1,16]{2,1,0:T(1,128)S(1)}, u32[]{:S(2)}, u32[]{:S(2)}) %all-to-all-start) | async-done | bytes 4128 | tf_op jit(solution)/shard_map/all_to_all | solution.py:56
  31.7 5.7 %all-to-all-start.1 = ((bf16[64,16,768]{2,1,0:T(8,128)(2,1)}), bf16[64,16,768]{2,1,0:T(8,128)(2,1)S(1)}, u32[]{:S(2)}, u32[]{:S(2)}) async-start(bf16[64,16,768]{2,1,0:T(8,128)(2,1)} %bitcast.30), calls=%async_computation.1 | async-start | bytes 3145728 | tf_op jit(solution)/shard_map/all_to_all | solution.py:53
  37.4 0.7 constant_dynamic-slice_fusion
  38.2 1.2 fusion.29
  39.4 0.5 broadcast.69
  39.9 0.7 reduce.3
  40.8 0.1 convert_reduce_fusion.1
  40.9 48.3 %all-reduce.3.cloned.1.call-done = f32[128,768]{1,0:T(8,128)} async-done(((f32[128,768]{1,0:T(8,128)}), f32[128,768]{1,0:T(8,128)}) %all-reduce.3.cloned.1.call-update) | async-done | bytes 393232 | tf_op jit(solution)/shard_map/psum | solution.py:67
  89.2 1.7 fusion.9
  91.0 0.7 fusion.3
  91.7 0.4 fusion.16
  92.1 1.1 convolution_add_fusion.2
  93.3 0.1 convert_reduce_fusion
  93.4 9.3 %psum.23 = f32[4]{0:T(128)S(1)} all-reduce(f32[4]{0:T(128)S(1)} %get-tuple-element.2), channel_id=1, replica_groups=mesh['shard'=64,'help'=4] {'help'}, use_global_device_ids=true, to_apply=%region_6.7 | all-reduce | flops 4 | bytes 32 | tf_op jit(solution)/shard_map/psum | solution.py:75
  102.8 38.5 %all-reduce.5.cloned.1.call-done = f32[128,768]{1,0:T(8,128)} async-done(((f32[128,768]{1,0:T(8,128)}), f32[128,768]{1,0:T(8,128)}) %all-reduce.5.cloned.1.call-update) | async-done | bytes 393232 | tf_op jit(solution)/shard_map/psum | solution.py:75
  141.3 1.7 fusion.21
  143.0 0.7 convolution_add_fusion
  143.7 0.1 select_reduce_fusion.2
  143.9 1.1 fusion
  145.0 0.6 dynamic_slice.7
  145.6 23.7 %reduce-scatter.2.cloned.1.call-done = f32[1,32,768]{2,1,0:T(8,128)} async-done(((f32[4,32,768]{2,1,0:T(8,128)}), f32[1,32,768]{2,1,0:T(8,128)}) %reduce-scatter.2.cloned.1.call-update) | async-done | bytes 98320 | tf_op jit(solution)/shard_map/reduce_scatter | solution.py:82
  169.3 2.2 %broadcast_multiply_fusion = f32[1,32,768]{2,1,0:T(8,128)} fusion(f32[1,32,768]{2,1,0:T(8,128)} %reduce-scatter.2.cloned.1.call-done, f32[]{:T(128)} %bitcast.13), kind=kLoop, calls=%fused_computation.42 | loop fusion | flops 24576 | bytes 196612 | tf_op jit(solution)/shard_map/mul | solution.py:86
  (29 shorter events, 0.5 us)
Async XLA Ops:
  7.2 31.0 %copy-start = (bf16[1024,768]{1,0:T(8,128)(2,1)S(1)}, bf16[1024,768]{1,0:T(8,128)(2,1)}, u32[]{:S(2)}) copy-start(bf16[1024,768]{1,0:T(8,128)(2,1)} %param.9) | copy-start | bytes 4718596
  11.3 20.3 %all-to-all-start = ((s32[64,1,16]{2,1,0:T(1,128)}), s32[64,1,16]{2,1,0:T(1,128)S(1)}, u32[]{:S(2)}, u32[]{:S(2)}) async-start(s32[64,1,16]{2,1,0:T(1,128)} %bitcast.5), calls=%async_computation | async-start | bytes 65536 | tf_op jit(solution)/shard_map/all_to_all | solution.py:56
  31.7 6.5 %copy-start.4 = (bf16[32,1024]{1,0:T(8,128)(2,1)S(1)}, bf16[32,1024]{1,0:T(8,128)(2,1)}, u32[]{:S(2)}) copy-start(bf16[32,1024]{1,0:T(8,128)(2,1)} %param.11) | copy-start | bytes 196612
  31.7 57.6 %all-to-all-start.1 = ((bf16[64,16,768]{2,1,0:T(8,128)(2,1)}), bf16[64,16,768]{2,1,0:T(8,128)(2,1)S(1)}, u32[]{:S(2)}, u32[]{:S(2)}) async-start(bf16[64,16,768]{2,1,0:T(8,128)(2,1)} %bitcast.30), calls=%async_computation.1 | async-start | bytes 3145728 | tf_op jit(solution)/shard_map/all_to_all | solution.py:53
  37.4 51.8 %all-reduce.3.cloned.1.call-start = ((), (), s32[]{:S(2)}) async-start(), calls=%async_computation.3 | async-start | bytes 786432 | tf_op jit(solution)/shard_map/psum | solution.py:67
  39.4 101.9 %all-reduce.5.cloned.1.call-start = ((), (), s32[]{:S(2)}) async-start(), calls=%async_computation.4 | async-start | bytes 786432 | tf_op jit(solution)/shard_map/psum | solution.py:75
  89.2 1.8 copy-start.1
  92.1 1.2 copy-start.5
  93.2 76.0 %reduce-scatter.2.cloned.1.call-start = ((), (), s32[]{:S(2)}) async-start(), calls=%async_computation.5 | async-start | bytes 491520 | tf_op jit(solution)/shard_map/reduce_scatter | solution.py:82
  141.3 1.7 copy-start.2
  143.8 27.6 %copy-start.3 = (f32[32,1024]{1,0:T(8,128)}, f32[32,1024]{1,0:T(8,128)S(1)}, u32[]{:S(2)}) copy-start(f32[32,1024]{1,0:T(8,128)S(1)} %select_reduce_fusion.2) | copy-start | bytes 393220
Sparse Core Ops, SparseCore 0:
  40.5 48.6 all-reduce.2
  93.4 47.9 all-reduce.4
  145.1 24.1 reduce-scatter.1

commit v2 on v1

v2 whole, which is shorter than its diff:
```python
import functools

import jax
import jax.numpy as jnp
from jax import lax
from jax.experimental import pallas as pl
from jax.experimental.pallas import tpu as pltpu
from jax.sharding import PartitionSpec as P

F32 = jnp.float32
BF16 = jnp.bfloat16
I32 = jnp.int32
MESH = pl.DeviceIdType.MESH
PLANE = 8
BACK = F32
FULL = F32
LAST = F32


def dot(a, b, ca, cb):
    return lax.dot_general(a, b, (((ca,), (cb,)), ((), ())), preferred_element_type=F32)


def stack_halves(v):
    hi = v.astype(BF16)
    lo = (v - hi.astype(F32)).astype(BF16)
    return jnp.concatenate([hi, lo], axis=0)


def dot_halves(v, w, cw):
    both = dot(stack_halves(v), w, 1, cw)
    n = v.shape[0]
    return both[:n] + both[n:]


def kernel(
    planes, helpers, capacity,
    group_hbm, local_hbm, query_hbm, point_hbm, cluster_hbm, test_hbm,
    sketch_hbm, regress_hbm,
    group, local, query, point, cluster, test,
    send, recv, tag_send, tag_recv,
    lead_part, lead_in, lead, count_part, count_in,
    back_part, back_in, back, last_part, last_in, sketch, regress,
    load_sem, row_send, row_recv, own_sem, tag_ssem, tag_rsem,
    lead_sem, lead2_sem, count_sem, back_sem, back2_sem, last_sem, out_sem,
):
    s = lax.axis_index("shard")
    h = lax.axis_index("help")
    z = s // PLANE
    spot = lax.rem(s, PLANE)
    groups = planes * PLANE
    rows, width = query.shape
    own_points = point.shape[0]
    rank = test.shape[0]
    slots = groups * capacity
    chunk = PLANE * capacity

    barrier = pltpu.get_barrier_semaphore()

    def greet(j, carry):
        pl.semaphore_signal(
            barrier, inc=1, device_id={"shard": lax.rem(s + j, groups)}, device_id_type=MESH
        )
        return carry

    lax.fori_loop(1, groups, greet, 0)
    for j in range(1, helpers):
        pl.semaphore_signal(
            barrier, inc=1, device_id={"help": lax.rem(h + j, helpers)}, device_id_type=MESH
        )

    loads = []
    for i, (a, b) in enumerate(
        ((group_hbm, group), (local_hbm, local), (query_hbm, query),
         (cluster_hbm, cluster), (test_hbm, test), (point_hbm, point))
    ):
        c = pltpu.make_async_copy(a, b, load_sem.at[i])
        c.start()
        loads.append(c)

    loads[0].wait()
    loads[1].wait()
    glabel = lax.broadcasted_iota(I32, (groups, rows), 0)
    hot = [glabel == group[k:k + 1, :] for k in range(2)]
    hotf = [m.astype(F32) for m in hot]
    earlier = (
        lax.broadcasted_iota(I32, (rows, rows), 0) < lax.broadcasted_iota(I32, (rows, rows), 1)
    ).astype(F32).astype(BF16)
    first_total = jnp.sum(hotf[0], axis=1, keepdims=True)
    before = [dot(hotf[k].astype(BF16), earlier, 1, 0) for k in range(2)]
    before[1] = before[1] + first_total
    order = [jnp.sum(hotf[k] * before[k], axis=0, keepdims=True).astype(I32) for k in range(2)]
    place = [group[k:k + 1, :] * capacity + order[k] for k in range(2)]
    lane = lax.broadcasted_iota(I32, (128, rows), 0)
    tags = sum(
        dot(
            (hotf[k] * (local[k:k + 1, :] + 1).astype(F32)).astype(BF16),
            (lane == order[k]).astype(F32).astype(BF16), 1, 1,
        )
        for k in range(2)
    )
    tag_send[...] = tags.reshape(groups, 1, 128)
    tag_recv[pl.ds(s, 1)] = tag_send[pl.ds(s, 1)]

    loads[2].wait()
    pl.semaphore_wait(barrier, groups - 1 + helpers - 1)

    def tag_copy(j, carry):
        t = lax.rem(s + j, groups)
        pltpu.make_async_remote_copy(
            src_ref=tag_send.at[t], dst_ref=tag_recv.at[s], send_sem=tag_ssem, recv_sem=tag_rsem,
            device_id={"shard": t}, device_id_type=MESH,
        ).start()
        return carry

    lax.fori_loop(1, groups, tag_copy, 0)

    far_first = sorted(range(planes), key=lambda d: -min(d, planes - d))
    slot = lax.broadcasted_iota(I32, (chunk, rows), 0)
    queries = query[...]
    for dz in far_first:
        zt = lax.rem(z + dz, planes)
        base = slot + zt * chunk
        pick = ((base == place[0]) | (base == place[1])).astype(F32).astype(BF16)
        packed = dot(pick, queries, 1, 0).astype(BF16)
        send[pl.ds(zt * PLANE, PLANE)] = packed.reshape(PLANE, capacity, width)

        def row_copy(e, carry, zt=zt, dz=dz):
            t = zt * PLANE + lax.rem(spot + e, PLANE)
            pltpu.make_async_remote_copy(
                src_ref=send.at[t], dst_ref=recv.at[s], send_sem=row_send, recv_sem=row_recv.at[dz],
                device_id={"shard": t}, device_id_type=MESH,
            ).start()
            return carry

        lax.fori_loop(1 if dz == 0 else 0, PLANE, row_copy, 0)
    own_copy = pltpu.make_async_copy(send.at[s], recv.at[s], own_sem)
    own_copy.start()

    def exchange(part, landing, sem):
        copies = []
        for j in range(1, helpers):
            t = lax.rem(h + j, helpers)
            copies.append(pltpu.make_async_remote_copy(
                src_ref=part.at[t], dst_ref=landing.at[j - 1],
                send_sem=sem.at[0, j - 1], recv_sem=sem.at[1, j - 1],
                device_id={"help": t}, device_id_type=MESH,
            ))
        for c in copies:
            c.start()
        return copies

    def publish(source, landing, sem):
        copies = []
        for j in range(1, helpers):
            t = lax.rem(h + j, helpers)
            copies.append(pltpu.make_async_remote_copy(
                src_ref=source, dst_ref=landing,
                send_sem=sem.at[0, j - 1], recv_sem=sem.at[1, j - 1],
                device_id={"help": t}, device_id_type=MESH,
            ))
        for c in copies:
            c.start()
        return copies

    def finish(copies):
        for c in copies:
            c.wait()

    for i in (3, 4, 5):
        loads[i].wait()
    mine = cluster[:, pl.ds(pl.multiple_of(h * own_points, own_points), own_points)]
    inside = [mine == c for c in range(helpers)]
    omega = test[...].astype(F32)
    spread = jnp.concatenate([jnp.where(m, omega, 0.0) for m in inside], axis=0).astype(BF16)
    lead_part[...] = dot(spread, point[...], 1, 0).reshape(helpers, rank, width)
    lead_copies = exchange(lead_part, lead_in, lead_sem)

    pltpu.make_async_remote_copy(
        src_ref=tag_send.at[pl.ds(0, groups - 1)], dst_ref=tag_recv.at[pl.ds(0, groups - 1)],
        send_sem=tag_ssem, recv_sem=tag_rsem,
        device_id={"shard": lax.rem(s + 1, groups)}, device_id_type=MESH,
    ).wait()
    tags = [tag_row(tag_recv, p, chunk, capacity) for p in range(planes)]
    named = [
        sum(jnp.sum((t == c + 1.0).astype(F32), axis=1, keepdims=True) for t in tags)
        for c in range(helpers)
    ]
    for c in range(helpers):
        count_part[c:c + 1, :] = jnp.broadcast_to(named[c], (1, 128))
    count_copies = []
    for j in range(1, helpers):
        c = pltpu.make_async_remote_copy(
            src_ref=count_part, dst_ref=count_in.at[j - 1],
            send_sem=count_sem.at[0, j - 1], recv_sem=count_sem.at[1, j - 1],
            device_id={"help": lax.rem(h + j, helpers)}, device_id_type=MESH,
        )
        c.start()
        count_copies.append(c)

    finish(lead_copies)
    total = lead_part[h]
    for j in range(helpers - 1):
        total = total + lead_in[j]
    lead[h] = total
    lead_copies = publish(lead.at[h], lead.at[h], lead2_sem)

    finish(count_copies)
    queried_all = count_part[...]
    for j in range(helpers - 1):
        queried_all = queried_all + count_in[j]
    everyone = cluster[...]
    factor = jnp.zeros((1, own_points), F32)
    for c in range(helpers):
        resident = jnp.sum((everyone == c).astype(F32), axis=1, keepdims=True)
        queried = queried_all[c:c + 1, 0:1]
        one = (1.0 / width) / jnp.sqrt((queried + 1.0) * (queried + resident))
        factor = jnp.where(inside[c], one, factor)
    own_resident = jnp.sum((everyone == h).astype(F32), axis=1, keepdims=True)
    own_scale = 1.0 / jnp.sqrt(own_resident)

    finish(lead_copies)
    halves = stack_halves(lead[...].reshape(helpers * rank, width))
    n = helpers * rank

    acc = jnp.zeros((2 * n, width), F32)
    for dz in sorted(range(planes), key=lambda d: min(d, planes - d)):
        zs = lax.rem(z + planes - dz, planes)
        k = PLANE - 1 if dz == 0 else PLANE
        pltpu.make_async_remote_copy(
            src_ref=send.at[pl.ds(0, k)], dst_ref=recv.at[pl.ds(0, k)],
            send_sem=row_send, recv_sem=row_recv.at[dz],
            device_id={"shard": lax.rem(s + 1, groups)}, device_id_type=MESH,
        ).wait_recv()
        if dz == 0:
            own_copy.wait()
        rowsy = recv[pl.ds(zs * PLANE, PLANE)].reshape(chunk, width)
        both = dot(halves, rowsy, 1, 1)
        lifted = both[:n] + both[n:]
        piece = tag_row(tag_recv, zs, chunk, capacity)
        lifted = jnp.concatenate(
            [jnp.where(piece == c + 1.0, lifted[c * rank:(c + 1) * rank], 0.0) for c in range(helpers)],
            axis=0,
        )
        acc = acc + dot(stack_halves(lifted), rowsy, 1, 0)
    product = (acc[:n] + acc[n:]).reshape(helpers, rank, width)
    back_part[...] = product.astype(BACK)
    back_copies = exchange(back_part, back_in, back_sem)
    finish(back_copies)
    total = back_part[h].astype(F32)
    for j in range(helpers - 1):
        total = total + back_in[j].astype(F32)
    back[h] = total.astype(FULL)
    finish(publish(back.at[h], back.at[h], back2_sem))

    full = back[...].reshape(n, width)
    points = point[...]
    if FULL == F32:
        wide = dot_halves(full, points, 1)
    else:
        wide = dot(full, points, 1, 1)
    chosen = wide[:rank]
    for c in range(1, helpers):
        chosen = jnp.where(inside[c], wide[c * rank:(c + 1) * rank], chosen)
    result = chosen * factor
    sketch[...] = result
    sketch_copy = pltpu.make_async_copy(sketch, sketch_hbm, out_sem.at[0])
    sketch_copy.start()
    rounded = result.astype(BF16).astype(F32)
    weighted = jnp.concatenate([jnp.where(m, rounded, 0.0) for m in inside], axis=0).astype(BF16)
    last_part[...] = dot(weighted, points, 1, 0).reshape(helpers, rank, width).astype(LAST)
    finish(exchange(last_part, last_in, last_sem))
    total = last_part[h].astype(F32)
    for j in range(helpers - 1):
        total = total + last_in[j].astype(F32)
    regress[...] = (total * own_scale).reshape(1, rank, width)
    regress_copy = pltpu.make_async_copy(regress, regress_hbm, out_sem.at[1])
    regress_copy.start()

    pltpu.make_async_remote_copy(
        src_ref=send.at[pl.ds(0, groups - 1)], dst_ref=recv.at[pl.ds(0, groups - 1)],
        send_sem=row_send, recv_sem=row_recv.at[0],
        device_id={"shard": lax.rem(s + 1, groups)}, device_id_type=MESH,
    ).wait_send()
    sketch_copy.wait()
    regress_copy.wait()


def tag_row(tag_recv, plane, chunk, capacity):
    part = tag_recv[pl.ds(plane * PLANE, PLANE)].reshape(PLANE, 128).astype(BF16)
    source = (
        lax.broadcasted_iota(I32, (PLANE, chunk), 0)
        == lax.broadcasted_iota(I32, (PLANE, chunk), 1) // capacity
    ).astype(F32).astype(BF16)
    wide = dot(part, source, 0, 0)[:capacity]
    return jnp.sum(
        jnp.where(
            lax.broadcasted_iota(I32, (capacity, chunk), 0)
            == lax.rem(lax.broadcasted_iota(I32, (capacity, chunk), 1), capacity),
            wide, 0.0,
        ),
        axis=0, keepdims=True,
    )


def shards(queries, probe_group, probe_local, points, point_cluster, test_matrix):
    groups = lax.axis_size("shard")
    helpers = lax.axis_size("help")
    rows, width = queries.shape
    probes = probe_group.shape[1]
    capacity = 2 * rows * probes // groups
    own_points = points.shape[0]
    rank = test_matrix.shape[0]
    planes = groups // PLANE
    peers = helpers - 1
    slab = (helpers, rank, width)
    away = (peers, rank, width)
    DMA = pltpu.SemaphoreType.DMA
    return pl.pallas_call(
        functools.partial(kernel, planes, helpers, capacity),
        out_shape=(
            jax.ShapeDtypeStruct((rank, own_points), F32),
            jax.ShapeDtypeStruct((1, rank, width), F32),
        ),
        in_specs=[pl.BlockSpec(memory_space=pl.ANY)] * 6,
        out_specs=(pl.BlockSpec(memory_space=pl.ANY), pl.BlockSpec(memory_space=pl.ANY)),
        scratch_shapes=[
            pltpu.VMEM((probes, rows), I32),
            pltpu.VMEM((probes, rows), I32),
            pltpu.VMEM((rows, width), BF16),
            pltpu.VMEM((own_points, width), BF16),
            pltpu.VMEM(point_cluster.shape, I32),
            pltpu.VMEM((rank, own_points), BF16),
            pltpu.VMEM((groups, capacity, width), BF16),
            pltpu.VMEM((groups, capacity, width), BF16),
            pltpu.VMEM((groups, 1, 128), F32),
            pltpu.VMEM((groups, 1, 128), F32),
            pltpu.VMEM(slab, F32),
            pltpu.VMEM(away, F32),
            pltpu.VMEM(slab, F32),
            pltpu.VMEM((helpers, 128), F32),
            pltpu.VMEM((peers, helpers, 128), F32),
            pltpu.VMEM(slab, BACK),
            pltpu.VMEM(away, BACK),
            pltpu.VMEM(slab, FULL),
            pltpu.VMEM(slab, LAST),
            pltpu.VMEM(away, LAST),
            pltpu.VMEM((rank, own_points), F32),
            pltpu.VMEM((1, rank, width), F32),
            DMA((6,)),
            DMA,
            DMA((planes,)),
            DMA,
            DMA,
            DMA,
            DMA((2, peers)),
            DMA((2, peers)),
            DMA((2, peers)),
            DMA((2, peers)),
            DMA((2, peers)),
            DMA((2, peers)),
            DMA((2,)),
        ],
        compiler_params=pltpu.CompilerParams(collective_id=0, has_side_effects=True),
    )(probe_group.T, probe_local.T, queries, points, point_cluster, test_matrix)


def solution(mesh):
    in_specs = (
        P(("shard", "help"), None),
        P(("shard", "help"), None),
        P(("shard", "help"), None),
        P(("shard", "help"), None),
        P("shard", None),
        P(None, ("shard", "help")),
    )
    out_specs = (P(None, ("shard", "help")), P(("shard", "help"), None, None))
    return jax.shard_map(shards, mesh=mesh, in_specs=in_specs, out_specs=out_specs, check_vma=False)
```

time: 179 us -> 77.7 us (0.43)
  waiting for transfers between devices: 116 us -> 0 us
  Pallas kernels: 0 us -> 73 us
  starting transfers between devices: 17.6 us -> 0 us
  between operations: 13.9 us -> 0.64 us
  matrix products: 11.6 us -> 0 us
  blocking collectives: 9.33 us -> 0 us
  other arithmetic: 5.17 us -> 0 us
    psum x2 -> x0, waiting for transfers between devices: 86.9 us -> none  [the longest x1 48.3 us: shards(): lead = lax.psum(jnp.dot(spread, points, preferred_element_type=F32), 'help')]
    pallas_call x0 -> x1, Pallas kernels: none -> 73 us  [shards(): pl.pallas_call(functools.partial(kernel, planes, helpers, capacity), out_...]
    reduce_scatter x1 -> x0, waiting for transfers between devices: 23.7 us -> none  [shards(): lax.psum_scatter(summed.reshape(clusters, rank, width), 'help', scatter_d...]
    all_to_all x2 -> x0, starting transfers between devices: 17.5 us -> none  [the longest x1 11.8 us: shards(): lax.all_to_all(ids.astype(jnp.int32).reshape(groups, 1, capacity), 'shard...]
    dot_general x10 -> x0, matrix products: 11.6 us -> none  [the longest x3 3.8 us: dot2(): lax.dot_general(hi, w, (dims, ((), ())), preferred_element_type=F32)]
    psum x1 -> x0, blocking collectives: 9.33 us -> none  [shards(): back, queried = lax.psum((back, named), 'help')]
    all_to_all x2 -> x0, waiting for transfers between devices: 5.81 us -> none  [the longest x1 5.81 us: shards(): lax.all_to_all(ids.astype(jnp.int32).reshape(groups, 1, capacity), 'shard...]
    mul x1 -> x0, other arithmetic: 2.17 us -> none  [shards(): return (sketch, own * own_scale[:, None, None])]
  transfers between devices with their start and end apart: 5 -> 0, of which waited for: 4 -> 0; matrix products, arithmetic and copies ran while one was open for 4% -> 0% of each run, Pallas kernels for 0% -> 0%
where the time goes in v2:
time: 77.7 us; the launch traced here: 76.8 us
  Pallas kernels  73 us (94%)
  local copies, waits for them, and re-layouts  3.11 us (4%)
    pallas_call x1, Pallas kernels, shards(): pl.pallas_call(functools.partial(kernel, planes, helpers, capacity), out_...  73 us
    unnamed x2, local copies, waits for them, and re-layouts  3.11 us

profile of v2, /device:TPU:32, one launch (start us, length us, event | category | flops | bytes accessed | tf_op | source)
XLA Modules:
  0.0 76.8 jit_solution(13422825880655025988)
XLA Ops:
  0.6 73.0 %shard_map.77 = (f32[32,1024]{1,0:T(8,128)}, f32[1,32,768]{2,1,0:T(8,128)}) custom-call(s32[2,256]{1,0:T(2,128)} %bitcast.2, s32[2,256]{1,0:T(2,128)} %bitcast.3, bf16[256,768]{1,0:T(8,128)(2,1)} %query_hbm.1, bf16[1024,768]{1,0:T(8,128)(2,1)} %point_hbm.1, s32[1,4096]{1,0:T(1,128)} %cluster_hbm.1, bf16[32,1024]{1,0:T(8,128)(2,1)} %test_hbm.1), custom_call_target="tpu_custom_call" | custom-call | tf_op jit(solution)/shard_map/pallas_call | solution.py:319
  73.7 1.6 %copy.10 = f32[32,1024]{1,0:T(8,128)} copy(f32[32,1024]{1,0:T(8,128)} %get-tuple-element.4) | data formatting | bytes 262144
  75.2 1.5 %copy.11 = f32[1,32,768]{2,1,0:T(8,128)} copy(f32[1,32,768]{2,1,0:T(8,128)} %get-tuple-element.5) | data formatting | bytes 196608

commit v3 on v2

--- a/solution.py
+++ b/solution.py
@@ -12,9 +12,9 @@
 I32 = jnp.int32
 MESH = pl.DeviceIdType.MESH
 PLANE = 8
-BACK = F32
-FULL = F32
-LAST = F32
+BACK = BF16
+FULL = BF16
+LAST = BF16
 
 
 def dot(a, b, ca, cb):
@@ -42,7 +42,7 @@
     lead_part, lead_in, lead, count_part, count_in,
     back_part, back_in, back, last_part, last_in, sketch, regress,
     load_sem, row_send, row_recv, own_sem, tag_ssem, tag_rsem,
-    lead_sem, lead2_sem, count_sem, back_sem, back2_sem, last_sem, out_sem,
+    lead_sem, lead2_sem, count_sem, back_sem, back2_sem, last_sem, out_sem, round_sem,
 ):
     s = lax.axis_index("shard")
     h = lax.axis_index("help")
@@ -57,13 +57,24 @@
 
     barrier = pltpu.get_barrier_semaphore()
 
+    column = sorted({1, planes - 1})
+
     def greet(j, carry):
         pl.semaphore_signal(
-            barrier, inc=1, device_id={"shard": lax.rem(s + j, groups)}, device_id_type=MESH
+            barrier, inc=1, device_id={"shard": z * PLANE + lax.rem(spot + j, PLANE)},
+            device_id_type=MESH,
         )
         return carry
 
-    lax.fori_loop(1, groups, greet, 0)
+    def call_column(ref):
+        for i, d in enumerate(column):
+            pl.semaphore_signal(
+                ref(i), inc=1, device_id={"shard": lax.rem(s + d * PLANE, groups)},
+                device_id_type=MESH,
+            )
+
+    call_column(lambda i: barrier)
+    lax.fori_loop(1, PLANE, greet, 0)
     for j in range(1, helpers):
         pl.semaphore_signal(
             barrier, inc=1, device_id={"help": lax.rem(h + j, helpers)}, device_id_type=MESH
@@ -103,37 +114,55 @@
     tag_recv[pl.ds(s, 1)] = tag_send[pl.ds(s, 1)]
 
     loads[2].wait()
-    pl.semaphore_wait(barrier, groups - 1 + helpers - 1)
-
-    def tag_copy(j, carry):
-        t = lax.rem(s + j, groups)
-        pltpu.make_async_remote_copy(
-            src_ref=tag_send.at[t], dst_ref=tag_recv.at[s], send_sem=tag_ssem, recv_sem=tag_rsem,
-            device_id={"shard": t}, device_id_type=MESH,
-        ).start()
-        return carry
-
-    lax.fori_loop(1, groups, tag_copy, 0)
-
-    far_first = sorted(range(planes), key=lambda d: -min(d, planes - d))
     slot = lax.broadcasted_iota(I32, (chunk, rows), 0)
     queries = query[...]
-    for dz in far_first:
+
+    def pack(dz):
         zt = lax.rem(z + dz, planes)
         base = slot + zt * chunk
         pick = ((base == place[0]) | (base == place[1])).astype(F32).astype(BF16)
         packed = dot(pick, queries, 1, 0).astype(BF16)
         send[pl.ds(zt * PLANE, PLANE)] = packed.reshape(PLANE, capacity, width)
 
-        def row_copy(e, carry, zt=zt, dz=dz):
+    def ship(dz):
+        zt = lax.rem(z + dz, planes)
+
+        def tag_copy(e, carry):
             t = zt * PLANE + lax.rem(spot + e, PLANE)
             pltpu.make_async_remote_copy(
-                src_ref=send.at[t], dst_ref=recv.at[s], send_sem=row_send, recv_sem=row_recv.at[dz],
+                src_ref=tag_send.at[t], dst_ref=tag_recv.at[s],
+                send_sem=tag_ssem, recv_sem=tag_rsem.at[dz],
                 device_id={"shard": t}, device_id_type=MESH,
             ).start()
             return carry
 
-        lax.fori_loop(1 if dz == 0 else 0, PLANE, row_copy, 0)
+        def row_copy(e, carry):
+            t = zt * PLANE + lax.rem(spot + e, PLANE)
+            pltpu.make_async_remote_copy(
+                src_ref=send.at[t], dst_ref=recv.at[s],
+                send_sem=row_send, recv_sem=row_recv.at[dz],
+                device_id={"shard": t}, device_id_type=MESH,
+            ).start()
+            return carry
+
+        low = 1 if dz == 0 else 0
+        lax.fori_loop(low, PLANE, tag_copy, 0)
+        lax.fori_loop(low, PLANE, row_copy, 0)
+
+    pack(0)
+    for d in column:
+        pack(d)
+    pl.semaphore_wait(barrier, len(column) + PLANE - 1 + helpers - 1)
+    for far in range(planes // 2 + 1):
+        if far > 0:
+            for i in range(len(column)):
+                pl.semaphore_wait(round_sem.at[far - 1, i], 1)
+        if far < planes // 2:
+            call_column(lambda i, far=far: round_sem.at[far, i])
+        for dz in sorted({far % planes, (planes - far) % planes}):
+            if far > 1:
+                pack(dz)
+            ship(dz)
     own_copy = pltpu.make_async_copy(send.at[s], recv.at[s], own_sem)
     own_copy.start()
 
@@ -176,16 +205,57 @@
     lead_part[...] = dot(spread, point[...], 1, 0).reshape(helpers, rank, width)
     lead_copies = exchange(lead_part, lead_in, lead_sem)
 
-    pltpu.make_async_remote_copy(
-        src_ref=tag_send.at[pl.ds(0, groups - 1)], dst_ref=tag_recv.at[pl.ds(0, groups - 1)],
-        send_sem=tag_ssem, recv_sem=tag_rsem,
-        device_id={"shard": lax.rem(s + 1, groups)}, device_id_type=MESH,
-    ).wait()
-    tags = [tag_row(tag_recv, p, chunk, capacity) for p in range(planes)]
-    named = [
-        sum(jnp.sum((t == c + 1.0).astype(F32), axis=1, keepdims=True) for t in tags)
-        for c in range(helpers)
+    finish(lead_copies)
+    total = lead_part[h]
+    for j in range(helpers - 1):
+        total = total + lead_in[j]
+    lead[h] = total
+    lead_copies = publish(lead.at[h], lead.at[h], lead2_sem)
+
+    everyone = cluster[...]
+    residents = [
+        jnp.sum((everyone == c).astype(F32), axis=1, keepdims=True) for c in range(helpers)
     ]
+    own_resident = jnp.sum((everyone == h).astype(F32), axis=1, keepdims=True)
+    own_scale = 1.0 / jnp.sqrt(own_resident)
+
+    finish(lead_copies)
+    halves = stack_halves(lead[...].reshape(helpers * rank, width))
+    n = helpers * rank
+
+    acc = jnp.zeros((2 * n, width), F32)
+    named = [jnp.zeros((1, 1), F32) for c in range(helpers)]
+    for dz in sorted(range(planes), key=lambda d: min(d, planes - d)):
+        zs = lax.rem(z + planes - dz, planes)
+        k = PLANE - 1 if dz == 0 else PLANE
+        pltpu.make_async_remote_copy(
+            src_ref=send.at[pl.ds(0, k)], dst_ref=recv.at[pl.ds(0, k)],
+            send_sem=row_send, recv_sem=row_recv.at[dz],
+            device_id={"shard": lax.rem(s + 1, groups)}, device_id_type=MESH,
+        ).wait_recv()
+        pltpu.make_async_remote_copy(
+            src_ref=tag_send.at[pl.ds(0, k)], dst_ref=tag_recv.at[pl.ds(0, k)],
+            send_sem=tag_ssem, recv_sem=tag_rsem.at[dz],
+            device_id={"shard": lax.rem(s + 1, groups)}, device_id_type=MESH,
+        ).wait_recv()
+        if dz == 0:
+            own_copy.wait()
+        rowsy = recv[pl.ds(zs * PLANE, PLANE)].reshape(chunk, width)
+        both = dot(halves, rowsy, 1, 1)
+        lifted = both[:n] + both[n:]
+        piece = tag_row(tag_recv, zs, chunk, capacity)
+        named = [
+            named[c] + jnp.sum((piece == c + 1.0).astype(F32), axis=1, keepdims=True)
+            for c in range(helpers)
+        ]
+        lifted = jnp.concatenate(
+            [jnp.where(piece == c + 1.0, lifted[c * rank:(c + 1) * rank], 0.0) for c in range(helpers)],
+            axis=0,
+        )
+        acc = acc + dot(stack_halves(lifted), rowsy, 1, 0)
+    product = (acc[:n] + acc[n:]).reshape(helpers, rank, width)
+    back_part[...] = product.astype(BACK)
+    back_copies = exchange(back_part, back_in, back_sem)
     for c in range(helpers):
         count_part[c:c + 1, :] = jnp.broadcast_to(named[c], (1, 128))
     count_copies = []
@@ -197,61 +267,22 @@
         )
         c.start()
         count_copies.append(c)
-
-    finish(lead_copies)
-    total = lead_part[h]
-    for j in range(helpers - 1):
-        total = total + lead_in[j]
-    lead[h] = total
-    lead_copies = publish(lead.at[h], lead.at[h], lead2_sem)
-
-    finish(count_copies)
-    queried_all = count_part[...]
-    for j in range(helpers - 1):
-        queried_all = queried_all + count_in[j]
-    everyone = cluster[...]
-    factor = jnp.zeros((1, own_points), F32)
-    for c in range(helpers):
-        resident = jnp.sum((everyone == c).astype(F32), axis=1, keepdims=True)
-        queried = queried_all[c:c + 1, 0:1]
-        one = (1.0 / width) / jnp.sqrt((queried + 1.0) * (queried + resident))
-        factor = jnp.where(inside[c], one, factor)
-    own_resident = jnp.sum((everyone == h).astype(F32), axis=1, keepdims=True)
-    own_scale = 1.0 / jnp.sqrt(own_resident)
-
-    finish(lead_copies)
-    halves = stack_halves(lead[...].reshape(helpers * rank, width))
-    n = helpers * rank
-
-    acc = jnp.zeros((2 * n, width), F32)
-    for dz in sorted(range(planes), key=lambda d: min(d, planes - d)):
-        zs = lax.rem(z + planes - dz, planes)
-        k = PLANE - 1 if dz == 0 else PLANE
-        pltpu.make_async_remote_copy(
-            src_ref=send.at[pl.ds(0, k)], dst_ref=recv.at[pl.ds(0, k)],
-            send_sem=row_send, recv_sem=row_recv.at[dz],
-            device_id={"shard": lax.rem(s + 1, groups)}, device_id_type=MESH,
-        ).wait_recv()
-        if dz == 0:
-            own_copy.wait()
-        rowsy = recv[pl.ds(zs * PLANE, PLANE)].reshape(chunk, width)
-        both = dot(halves, rowsy, 1, 1)
-        lifted = both[:n] + both[n:]
-        piece = tag_row(tag_recv, zs, chunk, capacity)
-        lifted = jnp.concatenate(
-            [jnp.where(piece == c + 1.0, lifted[c * rank:(c + 1) * rank], 0.0) for c in range(helpers)],
-            axis=0,
-        )
-        acc = acc + dot(stack_halves(lifted), rowsy, 1, 0)
-    product = (acc[:n] + acc[n:]).reshape(helpers, rank, width)
-    back_part[...] = product.astype(BACK)
-    back_copies = exchange(back_part, back_in, back_sem)
     finish(back_copies)
     total = back_part[h].astype(F32)
     for j in range(helpers - 1):
         total = total + back_in[j].astype(F32)
     back[h] = total.astype(FULL)
-    finish(publish(back.at[h], back.at[h], back2_sem))
+    back_copies = publish(back.at[h], back.at[h], back2_sem)
+    finish(count_copies)
+    queried_all = count_part[...]
+    for j in range(helpers - 1):
+        queried_all = queried_all + count_in[j]
+    factor = jnp.zeros((1, own_points), F32)
+    for c in range(helpers):
+        queried = queried_all[c:c + 1, 0:1]
+        one = (1.0 / width) / jnp.sqrt((queried + 1.0) * (queried + residents[c]))
+        factor = jnp.where(inside[c], one, factor)
+    finish(back_copies)
 
     full = back[...].reshape(n, width)
     points = point[...]
@@ -280,6 +311,11 @@
     pltpu.make_async_remote_copy(
         src_ref=send.at[pl.ds(0, groups - 1)], dst_ref=recv.at[pl.ds(0, groups - 1)],
         send_sem=row_send, recv_sem=row_recv.at[0],
+        device_id={"shard": lax.rem(s + 1, groups)}, device_id_type=MESH,
+    ).wait_send()
+    pltpu.make_async_remote_copy(
+        src_ref=tag_send.at[pl.ds(0, groups - 1)], dst_ref=tag_recv.at[pl.ds(0, groups - 1)],
+        send_sem=tag_ssem, recv_sem=tag_rsem.at[0],
         device_id={"shard": lax.rem(s + 1, groups)}, device_id_type=MESH,
     ).wait_send()
     sketch_copy.wait()
@@ -352,7 +388,7 @@
             DMA((planes,)),
             DMA,
             DMA,
-            DMA,
+            DMA((planes,)),
             DMA((2, peers)),
             DMA((2, peers)),
             DMA((2, peers)),
@@ -360,6 +396,7 @@
             DMA((2, peers)),
             DMA((2, peers)),
             DMA((2,)),
+            pltpu.SemaphoreType.REGULAR((planes // 2, 2)),
         ],
         compiler_params=pltpu.CompilerParams(collective_id=0, has_side_effects=True),
     )(probe_group.T, probe_local.T, queries, points, point_cluster, test_matrix)

time: 77.7 us -> 67.8 us (0.87)
  Pallas kernels: 73 us -> 63.9 us
    pallas_call x1, Pallas kernels: 73 us -> 63.9 us  [shards(): pl.pallas_call(functools.partial(kernel, planes, helpers, capacity), out_...]
where the time goes in v3:
time: 67.8 us; the launch traced here: 67.6 us
  Pallas kernels  63.9 us (94%)
  local copies, waits for them, and re-layouts  3.11 us (5%)
    pallas_call x1, Pallas kernels, shards(): pl.pallas_call(functools.partial(kernel, planes, helpers, capacity), out_...  63.9 us
    unnamed x2, local copies, waits for them, and re-layouts  3.11 us

profile of v3, /device:TPU:32, one launch (start us, length us, event | category | flops | bytes accessed | tf_op | source)
XLA Modules:
  0.0 67.6 jit_solution(10371659110705937098)
XLA Ops:
  0.6 63.9 %shard_map.77 = (f32[32,1024]{1,0:T(8,128)}, f32[1,32,768]{2,1,0:T(8,128)}) custom-call(s32[2,256]{1,0:T(2,128)} %bitcast.2, s32[2,256]{1,0:T(2,128)} %bitcast.3, bf16[256,768]{1,0:T(8,128)(2,1)} %query_hbm.1, bf16[1024,768]{1,0:T(8,128)(2,1)} %point_hbm.1, s32[1,4096]{1,0:T(1,128)} %cluster_hbm.1, bf16[32,1024]{1,0:T(8,128)(2,1)} %test_hbm.1), custom_call_target="tpu_custom_call" | custom-call | tf_op jit(solution)/shard_map/pallas_call | solution.py:355
  64.5 1.6 %copy.10 = f32[32,1024]{1,0:T(8,128)} copy(f32[32,1024]{1,0:T(8,128)} %get-tuple-element.4) | data formatting | bytes 262144
  66.1 1.5 %copy.11 = f32[1,32,768]{2,1,0:T(8,128)} copy(f32[1,32,768]{2,1,0:T(8,128)} %get-tuple-element.5) | data formatting | bytes 196608

commit v4 on v3

--- a/solution.py
+++ b/solution.py
@@ -43,6 +43,8 @@
     back_part, back_in, back, last_part, last_in, sketch, regress,
     load_sem, row_send, row_recv, own_sem, tag_ssem, tag_rsem,
     lead_sem, lead2_sem, count_sem, back_sem, back2_sem, last_sem, out_sem, round_sem,
+    far_rows, far_tags, far_lead, far_back, far_count,
+    share_sem, stag_sem, flead_sem, fback_sem, fcount_sem,
 ):
     s = lax.axis_index("shard")
     h = lax.axis_index("help")
@@ -111,7 +113,11 @@
         for k in range(2)
     )
     tag_send[...] = tags.reshape(groups, 1, 128)
+    opposite = planes // 2
+    zo = lax.rem(z + opposite, planes)
+    across = zo * PLANE + spot
     tag_recv[pl.ds(s, 1)] = tag_send[pl.ds(s, 1)]
+    tag_recv[pl.ds(across, 1)] = tag_send[pl.ds(across, 1)]
 
     loads[2].wait()
     slot = lax.broadcasted_iota(I32, (chunk, rows), 0)
@@ -126,45 +132,66 @@
 
     def ship(dz):
         zt = lax.rem(z + dz, planes)
+        zd = z if dz == opposite else zt
+        slot_there = across if dz == opposite else s
 
         def tag_copy(e, carry):
-            t = zt * PLANE + lax.rem(spot + e, PLANE)
+            t = lax.rem(spot + e, PLANE)
             pltpu.make_async_remote_copy(
-                src_ref=tag_send.at[t], dst_ref=tag_recv.at[s],
+                src_ref=tag_send.at[zt * PLANE + t], dst_ref=tag_recv.at[slot_there],
                 send_sem=tag_ssem, recv_sem=tag_rsem.at[dz],
-                device_id={"shard": t}, device_id_type=MESH,
+                device_id={"shard": zd * PLANE + t}, device_id_type=MESH,
             ).start()
             return carry
 
         def row_copy(e, carry):
-            t = zt * PLANE + lax.rem(spot + e, PLANE)
+            t = lax.rem(spot + e, PLANE)
             pltpu.make_async_remote_copy(
-                src_ref=send.at[t], dst_ref=recv.at[s],
+                src_ref=send.at[zt * PLANE + t], dst_ref=recv.at[slot_there],
                 send_sem=row_send, recv_sem=row_recv.at[dz],
-                device_id={"shard": t}, device_id_type=MESH,
+                device_id={"shard": zd * PLANE + t}, device_id_type=MESH,
             ).start()
             return carry
 
-        low = 1 if dz == 0 else 0
+        low = 1 if dz in (0, opposite) else 0
         lax.fori_loop(low, PLANE, tag_copy, 0)
         lax.fori_loop(low, PLANE, row_copy, 0)
 
     pack(0)
-    for d in column:
+    pack(opposite)
+    near = [d for d in column if d != opposite]
+    for d in near:
         pack(d)
     pl.semaphore_wait(barrier, len(column) + PLANE - 1 + helpers - 1)
-    for far in range(planes // 2 + 1):
-        if far > 0:
-            for i in range(len(column)):
-                pl.semaphore_wait(round_sem.at[far - 1, i], 1)
-        if far < planes // 2:
-            call_column(lambda i, far=far: round_sem.at[far, i])
-        for dz in sorted({far % planes, (planes - far) % planes}):
-            if far > 1:
-                pack(dz)
-            ship(dz)
-    own_copy = pltpu.make_async_copy(send.at[s], recv.at[s], own_sem)
+    call_column(lambda i: round_sem.at[0, i])
+    ship(0)
+    ship(opposite)
+    own_copy = pltpu.make_async_copy(send.at[s], recv.at[s], own_sem.at[0])
     own_copy.start()
+    across_copy = pltpu.make_async_copy(send.at[across], recv.at[across], own_sem.at[1])
+    across_copy.start()
+
+    def advance(far):
+        for i in range(len(column)):
+            pl.semaphore_wait(round_sem.at[far - 1, i], 1)
+        if far < opposite:
+            call_column(lambda i: round_sem.at[far, i])
+
+    def arrived(dz, k):
+        pltpu.make_async_remote_copy(
+            src_ref=send.at[pl.ds(0, k)], dst_ref=recv.at[pl.ds(0, k)],
+            send_sem=row_send, recv_sem=row_recv.at[dz],
+            device_id={"shard": lax.rem(s + 1, groups)}, device_id_type=MESH,
+        ).wait_recv()
+        pltpu.make_async_remote_copy(
+            src_ref=tag_send.at[pl.ds(0, k)], dst_ref=tag_recv.at[pl.ds(0, k)],
+            send_sem=tag_ssem, recv_sem=tag_rsem.at[dz],
+            device_id={"shard": lax.rem(s + 1, groups)}, device_id_type=MESH,
+        ).wait_recv()
+
+    advance(1)
+    for d in near:
+        ship(d)
 
     def exchange(part, landing, sem):
         copies = []
@@ -205,12 +232,52 @@
     lead_part[...] = dot(spread, point[...], 1, 0).reshape(helpers, rank, width)
     lead_copies = exchange(lead_part, lead_in, lead_sem)
 
+    for far in range(2, opposite + 1):
+        advance(far)
+        if far < opposite:
+            for dz in (far, planes - far):
+                pack(dz)
+                if far < opposite - 1 or far == 2:
+                    ship(dz)
+
+    def to_opposite(pair, sem):
+        c = pltpu.make_async_remote_copy(
+            src_ref=pair.at[0], dst_ref=pair.at[1], send_sem=sem.at[0], recv_sem=sem.at[1],
+            device_id={"shard": across}, device_id_type=MESH,
+        )
+        c.start()
+        return c
+
+    arrived(opposite, PLANE - 1)
+    across_copy.wait()
+    shared = []
+    for j in range(1, helpers):
+        for a, b, sem in ((recv, far_rows, share_sem), (tag_recv, far_tags, stag_sem)):
+            c = pltpu.make_async_remote_copy(
+                src_ref=a.at[pl.ds(zo * PLANE, PLANE)], dst_ref=b.at[j - 1],
+                send_sem=sem.at[0, j - 1], recv_sem=sem.at[1, j - 1],
+                device_id={"help": lax.rem(h + j, helpers)}, device_id_type=MESH,
+            )
+            c.start()
+            shared.append(c)
+    far_piece = tag_row(tag_recv[pl.ds(zo * PLANE, PLANE)], chunk, capacity)
+    for c in range(helpers):
+        far_count[0, c:c + 1, :] = jnp.broadcast_to(
+            jnp.sum((far_piece == c + 1.0).astype(F32), axis=1, keepdims=True), (1, 128)
+        )
+    count_move = to_opposite(far_count, fcount_sem)
+
     finish(lead_copies)
     total = lead_part[h]
     for j in range(helpers - 1):
         total = total + lead_in[j]
+    far_lead[0] = total.astype(BF16)
     lead[h] = total
+    lead_move = to_opposite(far_lead, flead_sem)
     lead_copies = publish(lead.at[h], lead.at[h], lead2_sem)
+    if opposite - 1 > 2:
+        for dz in (opposite - 1, opposite + 1):
+            ship(dz)
 
     everyone = cluster[...]
     residents = [
@@ -225,25 +292,36 @@
 
     acc = jnp.zeros((2 * n, width), F32)
     named = [jnp.zeros((1, 1), F32) for c in range(helpers)]
-    for dz in sorted(range(planes), key=lambda d: min(d, planes - d)):
+
+    def far_product():
+        lead_move.wait()
+        finish(shared)
+        lead_there = far_lead[1]
+        label = h.astype(F32) + 1.0
+        got = jnp.zeros((2 * rank, width), F32)
+        for j in range(helpers):
+            if j == 0:
+                far_r, piece = recv[pl.ds(zo * PLANE, PLANE)], far_piece
+            else:
+                far_r, piece = far_rows[j - 1], tag_row(far_tags[j - 1], chunk, capacity)
+            far_r = far_r.reshape(chunk, width)
+            lifted = jnp.where(piece == label, dot(lead_there, far_r, 1, 1), 0.0)
+            got = got + dot(stack_halves(lifted), far_r, 1, 0)
+        far_back[0] = (got[:rank] + got[rank:]).astype(BF16)
+        return to_opposite(far_back, fback_sem)
+
+    back_move = None
+    for dz in sorted([d for d in range(planes) if d != opposite], key=lambda d: min(d, planes - d)):
+        if back_move is None and min(dz, planes - dz) == max(opposite - 1, 1):
+            back_move = far_product()
         zs = lax.rem(z + planes - dz, planes)
-        k = PLANE - 1 if dz == 0 else PLANE
-        pltpu.make_async_remote_copy(
-            src_ref=send.at[pl.ds(0, k)], dst_ref=recv.at[pl.ds(0, k)],
-            send_sem=row_send, recv_sem=row_recv.at[dz],
-            device_id={"shard": lax.rem(s + 1, groups)}, device_id_type=MESH,
-        ).wait_recv()
-        pltpu.make_async_remote_copy(
-            src_ref=tag_send.at[pl.ds(0, k)], dst_ref=tag_recv.at[pl.ds(0, k)],
-            send_sem=tag_ssem, recv_sem=tag_rsem.at[dz],
-            device_id={"shard": lax.rem(s + 1, groups)}, device_id_type=MESH,
-        ).wait_recv()
+        arrived(dz, PLANE - 1 if dz == 0 else PLANE)
         if dz == 0:
             own_copy.wait()
         rowsy = recv[pl.ds(zs * PLANE, PLANE)].reshape(chunk, width)
         both = dot(halves, rowsy, 1, 1)
         lifted = both[:n] + both[n:]
-        piece = tag_row(tag_recv, zs, chunk, capacity)
+        piece = tag_row(tag_recv[pl.ds(zs * PLANE, PLANE)], chunk, capacity)
         named = [
             named[c] + jnp.sum((piece == c + 1.0).astype(F32), axis=1, keepdims=True)
             for c in range(helpers)
@@ -253,11 +331,14 @@
             axis=0,
         )
         acc = acc + dot(stack_halves(lifted), rowsy, 1, 0)
+    if back_move is None:
+        back_move = far_product()
+    count_move.wait()
     product = (acc[:n] + acc[n:]).reshape(helpers, rank, width)
     back_part[...] = product.astype(BACK)
     back_copies = exchange(back_part, back_in, back_sem)
     for c in range(helpers):
-        count_part[c:c + 1, :] = jnp.broadcast_to(named[c], (1, 128))
+        count_part[c:c + 1, :] = far_count[1, c:c + 1, :] + named[c]
     count_copies = []
     for j in range(1, helpers):
         c = pltpu.make_async_remote_copy(
@@ -268,7 +349,8 @@
         c.start()
         count_copies.append(c)
     finish(back_copies)
-    total = back_part[h].astype(F32)
+    back_move.wait()
+    total = back_part[h].astype(F32) + far_back[1].astype(F32)
     for j in range(helpers - 1):
         total = total + back_in[j].astype(F32)
     back[h] = total.astype(FULL)
@@ -308,13 +390,14 @@
     regress_copy = pltpu.make_async_copy(regress, regress_hbm, out_sem.at[1])
     regress_copy.start()
 
+    moved = 2 * (PLANE - 1) + (planes - 2) * PLANE
     pltpu.make_async_remote_copy(
-        src_ref=send.at[pl.ds(0, groups - 1)], dst_ref=recv.at[pl.ds(0, groups - 1)],
+        src_ref=send.at[pl.ds(0, moved)], dst_ref=recv.at[pl.ds(0, moved)],
         send_sem=row_send, recv_sem=row_recv.at[0],
         device_id={"shard": lax.rem(s + 1, groups)}, device_id_type=MESH,
     ).wait_send()
     pltpu.make_async_remote_copy(
-        src_ref=tag_send.at[pl.ds(0, groups - 1)], dst_ref=tag_recv.at[pl.ds(0, groups - 1)],
+        src_ref=tag_send.at[pl.ds(0, moved)], dst_ref=tag_recv.at[pl.ds(0, moved)],
         send_sem=tag_ssem, recv_sem=tag_rsem.at[0],
         device_id={"shard": lax.rem(s + 1, groups)}, device_id_type=MESH,
     ).wait_send()
@@ -322,8 +405,8 @@
     regress_copy.wait()
 
 
-def tag_row(tag_recv, plane, chunk, capacity):
-    part = tag_recv[pl.ds(plane * PLANE, PLANE)].reshape(PLANE, 128).astype(BF16)
+def tag_row(tags, chunk, capacity):
+    part = tags.reshape(PLANE, 128).astype(BF16)
     source = (
         lax.broadcasted_iota(I32, (PLANE, chunk), 0)
         == lax.broadcasted_iota(I32, (PLANE, chunk), 1) // capacity
@@ -386,7 +469,7 @@
             DMA((6,)),
             DMA,
             DMA((planes,)),
-            DMA,
+            DMA((2,)),
             DMA,
             DMA((planes,)),
             DMA((2, peers)),
@@ -397,6 +480,16 @@
             DMA((2, peers)),
             DMA((2,)),
             pltpu.SemaphoreType.REGULAR((planes // 2, 2)),
+            pltpu.VMEM((peers, PLANE, capacity, width), BF16),
+            pltpu.VMEM((peers, PLANE, 1, 128), F32),
+            pltpu.VMEM((2, rank, width), BF16),
+            pltpu.VMEM((2, rank, width), BF16),
+            pltpu.VMEM((2, helpers, 128), F32),
+            DMA((2, peers)),
+            DMA((2, peers)),
+            DMA((2,)),
+            DMA((2,)),
+            DMA((2,)),
         ],
         compiler_params=pltpu.CompilerParams(collective_id=0, has_side_effects=True),
     )(probe_group.T, probe_local.T, queries, points, point_cluster, test_matrix)

time: 67.8 us -> 61.9 us (0.913)
  Pallas kernels: 63.9 us -> 58 us
    pallas_call x1, Pallas kernels: 63.9 us -> 58 us  [shards(): pl.pallas_call(functools.partial(kernel, planes, helpers, capacity), out_...]
where the time goes in v4:
time: 61.9 us; the launch traced here: 61.8 us
  Pallas kernels  58 us (94%)
  local copies, waits for them, and re-layouts  3.11 us (5%)
  between operations  0.64 us (1%)
    pallas_call x1, Pallas kernels, shards(): pl.pallas_call(functools.partial(kernel, planes, helpers, capacity), out_...  58 us
    unnamed x2, local copies, waits for them, and re-layouts  3.11 us

profile of v4, /device:TPU:32, one launch (start us, length us, event | category | flops | bytes accessed | tf_op | source)
XLA Modules:
  0.0 61.8 jit_solution(11997325491163791934)
XLA Ops:
  0.6 58.0 %shard_map.77 = (f32[32,1024]{1,0:T(8,128)}, f32[1,32,768]{2,1,0:T(8,128)}) custom-call(s32[2,256]{1,0:T(2,128)} %bitcast.2, s32[2,256]{1,0:T(2,128)} %bitcast.3, bf16[256,768]{1,0:T(8,128)(2,1)} %query_hbm.1, bf16[1024,768]{1,0:T(8,128)(2,1)} %point_hbm.1, s32[1,4096]{1,0:T(1,128)} %cluster_hbm.1, bf16[32,1024]{1,0:T(8,128)(2,1)} %test_hbm.1), custom_call_target="tpu_custom_call" | custom-call | tf_op jit(solution)/shard_map/pallas_call | solution.py:438
  58.7 1.6 %copy.10 = f32[32,1024]{1,0:T(8,128)} copy(f32[32,1024]{1,0:T(8,128)} %get-tuple-element.4) | data formatting | bytes 262144
  60.2 1.5 %copy.11 = f32[1,32,768]{2,1,0:T(8,128)} copy(f32[1,32,768]{2,1,0:T(8,128)} %get-tuple-element.5) | data formatting | bytes 196608

commit v5 on v4

--- a/solution.py
+++ b/solution.py
@@ -56,6 +56,8 @@
     rank = test.shape[0]
     slots = groups * capacity
     chunk = PLANE * capacity
+    pieces, _, _, part_width = back.shape
+    cut = [slice(i * part_width, (i + 1) * part_width) for i in range(pieces)]
 
     barrier = pltpu.get_barrier_semaphore()
 
@@ -334,9 +336,11 @@
     if back_move is None:
         back_move = far_product()
     count_move.wait()
-    product = (acc[:n] + acc[n:]).reshape(helpers, rank, width)
-    back_part[...] = product.astype(BACK)
-    back_copies = exchange(back_part, back_in, back_sem)
+    product = acc[:n] + acc[n:]
+    back_copies = []
+    for i in range(pieces):
+        back_part[i] = product[:, cut[i]].reshape(helpers, rank, part_width).astype(BACK)
+        back_copies.append(exchange(back_part.at[i], back_in.at[i], back_sem.at[i]))
     for c in range(helpers):
         count_part[c:c + 1, :] = far_count[1, c:c + 1, :] + named[c]
     count_copies = []
@@ -348,13 +352,15 @@
         )
         c.start()
         count_copies.append(c)
-    finish(back_copies)
     back_move.wait()
-    total = back_part[h].astype(F32) + far_back[1].astype(F32)
-    for j in range(helpers - 1):
-        total = total + back_in[j].astype(F32)
-    back[h] = total.astype(FULL)
-    back_copies = publish(back.at[h], back.at[h], back2_sem)
+    full_copies = []
+    for i in range(pieces):
+        finish(back_copies[i])
+        total = back_part[i, h].astype(F32) + far_back[1, :, cut[i]].astype(F32)
+        for j in range(helpers - 1):
+            total = total + back_in[i, j].astype(F32)
+        back[i, h] = total.astype(FULL)
+        full_copies.append(publish(back.at[i, h], back.at[i, h], back2_sem.at[i]))
     finish(count_copies)
     queried_all = count_part[...]
     for j in range(helpers - 1):
@@ -364,14 +370,14 @@
         queried = queried_all[c:c + 1, 0:1]
         one = (1.0 / width) / jnp.sqrt((queried + 1.0) * (queried + residents[c]))
         factor = jnp.where(inside[c], one, factor)
-    finish(back_copies)
-
-    full = back[...].reshape(n, width)
-    points = point[...]
-    if FULL == F32:
-        wide = dot_halves(full, points, 1)
-    else:
-        wide = dot(full, points, 1, 1)
+    wide = jnp.zeros((n, own_points), F32)
+    for i in range(pieces):
+        finish(full_copies[i])
+        full = back[i].reshape(n, part_width)
+        if FULL == F32:
+            wide = wide + dot_halves(full, point[:, cut[i]], 1)
+        else:
+            wide = wide + dot(full, point[:, cut[i]], 1, 1)
     chosen = wide[:rank]
     for c in range(1, helpers):
         chosen = jnp.where(inside[c], wide[c * rank:(c + 1) * rank], chosen)
@@ -381,12 +387,17 @@
     sketch_copy.start()
     rounded = result.astype(BF16).astype(F32)
     weighted = jnp.concatenate([jnp.where(m, rounded, 0.0) for m in inside], axis=0).astype(BF16)
-    last_part[...] = dot(weighted, points, 1, 0).reshape(helpers, rank, width).astype(LAST)
-    finish(exchange(last_part, last_in, last_sem))
-    total = last_part[h].astype(F32)
-    for j in range(helpers - 1):
-        total = total + last_in[j].astype(F32)
-    regress[...] = (total * own_scale).reshape(1, rank, width)
+    last_copies = []
+    for i in range(pieces):
+        last = dot(weighted, point[:, cut[i]], 1, 0)
+        last_part[i] = last.reshape(helpers, rank, part_width).astype(LAST)
+        last_copies.append(exchange(last_part.at[i], last_in.at[i], last_sem.at[i]))
+    for i in range(pieces):
+        finish(last_copies[i])
+        total = last_part[i, h].astype(F32)
+        for j in range(helpers - 1):
+            total = total + last_in[i, j].astype(F32)
+        regress[0, :, cut[i]] = total * own_scale
     regress_copy = pltpu.make_async_copy(regress, regress_hbm, out_sem.at[1])
     regress_copy.start()
 
@@ -422,6 +433,20 @@
     )
 
 
+def deliver(a_ref, b_ref, a_out, b_out, a_buf, b_buf, sem):
+    moves = [
+        (pltpu.make_async_copy(a_ref, a_buf, sem.at[0]), pltpu.make_async_copy(a_buf, a_out, sem.at[1])),
+        (pltpu.make_async_copy(b_ref, b_buf, sem.at[2]), pltpu.make_async_copy(b_buf, b_out, sem.at[3])),
+    ]
+    for into, out in moves:
+        into.start()
+    for into, out in moves:
+        into.wait()
+        out.start()
+    for into, out in moves:
+        out.wait()
+
+
 def shards(queries, probe_group, probe_local, points, point_cluster, test_matrix):
     groups = lax.axis_size("shard")
     helpers = lax.axis_size("help")
@@ -432,10 +457,13 @@
     rank = test_matrix.shape[0]
     planes = groups // PLANE
     peers = helpers - 1
+    pieces = 3 if width % 384 == 0 else 1
     slab = (helpers, rank, width)
+    slabs = (pieces, helpers, rank, width // pieces)
+    aways = (pieces, peers, rank, width // pieces)
     away = (peers, rank, width)
     DMA = pltpu.SemaphoreType.DMA
-    return pl.pallas_call(
+    made = pl.pallas_call(
         functools.partial(kernel, planes, helpers, capacity),
         out_shape=(
             jax.ShapeDtypeStruct((rank, own_points), F32),
@@ -459,11 +487,11 @@
             pltpu.VMEM(slab, F32),
             pltpu.VMEM((helpers, 128), F32),
             pltpu.VMEM((peers, helpers, 128), F32),
-            pltpu.VMEM(slab, BACK),
-            pltpu.VMEM(away, BACK),
-            pltpu.VMEM(slab, FULL),
-            pltpu.VMEM(slab, LAST),
-            pltpu.VMEM(away, LAST),
+            pltpu.VMEM(slabs, BACK),
+            pltpu.VMEM(aways, BACK),
+            pltpu.VMEM(slabs, FULL),
+            pltpu.VMEM(slabs, LAST),
+            pltpu.VMEM(aways, LAST),
             pltpu.VMEM((rank, own_points), F32),
             pltpu.VMEM((1, rank, width), F32),
             DMA((6,)),
@@ -475,9 +503,9 @@
             DMA((2, peers)),
             DMA((2, peers)),
             DMA((2, peers)),
-            DMA((2, peers)),
-            DMA((2, peers)),
-            DMA((2, peers)),
+            DMA((pieces, 2, peers)),
+            DMA((pieces, 2, peers)),
+            DMA((pieces, 2, peers)),
             DMA((2,)),
             pltpu.SemaphoreType.REGULAR((planes // 2, 2)),
             pltpu.VMEM((peers, PLANE, capacity, width), BF16),
@@ -493,6 +521,17 @@
         ],
         compiler_params=pltpu.CompilerParams(collective_id=0, has_side_effects=True),
     )(probe_group.T, probe_local.T, queries, points, point_cluster, test_matrix)
+    sketch_shape, regress_shape = (rank, own_points), (1, rank, width)
+    return pl.pallas_call(
+        deliver,
+        out_shape=(
+            jax.ShapeDtypeStruct(sketch_shape, F32),
+            jax.ShapeDtypeStruct(regress_shape, F32),
+        ),
+        in_specs=[pl.BlockSpec(memory_space=pl.ANY)] * 2,
+        out_specs=(pl.BlockSpec(memory_space=pl.ANY), pl.BlockSpec(memory_space=pl.ANY)),
+        scratch_shapes=[pltpu.VMEM(sketch_shape, F32), pltpu.VMEM(regress_shape, F32), DMA((4,))],
+    )(*made)
 
 
 def solution(mesh):

time: 61.9 us -> 59.7 us (0.964)
  local copies, waits for them, and re-layouts: 3.11 us -> 0 us
  Pallas kernels: 58 us -> 59 us
    unnamed x2 -> x0, local copies, waits for them, and re-layouts: 3.11 us -> none
    pallas_call x0 -> x1, Pallas kernels: none -> 1.63 us  [shards(): pl.pallas_call(deliver, out_shape=(jax.ShapeDtypeStruct(sketch_shape, F32...]
    pallas_call x1, Pallas kernels: 58 us -> 57.3 us  [shards(): pl.pallas_call(functools.partial(kernel, planes, helpers, capacity), out_...]
where the time goes in v5:
time: 59.7 us; the launch traced here: 59.6 us
  Pallas kernels  59 us (99%)
  between operations  0.64 us (1%)
    pallas_call x1, Pallas kernels, shards(): pl.pallas_call(functools.partial(kernel, planes, helpers, capacity), out_...  57.3 us
    pallas_call x1, Pallas kernels, shards(): pl.pallas_call(deliver, out_shape=(jax.ShapeDtypeStruct(sketch_shape, F32...  1.63 us

profile of v5, /device:TPU:32, one launch (start us, length us, event | category | flops | bytes accessed | tf_op | source)
XLA Modules:
  0.0 59.6 jit_solution(14333873026908321027)
XLA Ops:
  0.6 57.3 %shard_map.77 = (f32[32,1024]{1,0:T(8,128)}, f32[1,32,768]{2,1,0:T(8,128)}) custom-call(s32[2,256]{1,0:T(2,128)} %bitcast.2, s32[2,256]{1,0:T(2,128)} %bitcast.3, bf16[256,768]{1,0:T(8,128)(2,1)} %query_hbm.1, bf16[1024,768]{1,0:T(8,128)(2,1)} %point_hbm.1, s32[1,4096]{1,0:T(1,128)} %cluster_hbm.1, bf16[32,1024]{1,0:T(8,128)(2,1)} %test_hbm.1), custom_call_target="tpu_custom_call" | custom-call | tf_op jit(solution)/shard_map/pallas_call | solution.py:466
  58.0 1.6 %shard_map.78 = (f32[32,1024]{1,0:T(8,128)}, f32[1,32,768]{2,1,0:T(8,128)}) custom-call(f32[32,1024]{1,0:T(8,128)} %get-tuple-element.4.a_ref, f32[1,32,768]{2,1,0:T(8,128)} %get-tuple-element.5.b_ref), custom_call_target="tpu_custom_call" | custom-call | tf_op jit(solution)/shard_map/pallas_call | solution.py:525

commit v6 on v5

--- a/solution.py
+++ b/solution.py
@@ -204,8 +204,8 @@
                 send_sem=sem.at[0, j - 1], recv_sem=sem.at[1, j - 1],
                 device_id={"help": t}, device_id_type=MESH,
             ))
-        for c in copies:
-            c.start()
+        for i in sorted(range(helpers - 1), key=lambda i: -min(i + 1, helpers - 1 - i)):
+            copies[i].start()
         return copies
 
     def publish(source, landing, sem):
@@ -217,8 +217,8 @@
                 send_sem=sem.at[0, j - 1], recv_sem=sem.at[1, j - 1],
                 device_id={"help": t}, device_id_type=MESH,
             ))
-        for c in copies:
-            c.start()
+        for i in sorted(range(helpers - 1), key=lambda i: -min(i + 1, helpers - 1 - i)):
+            copies[i].start()
         return copies
 
     def finish(copies):
@@ -314,7 +314,7 @@
 
     back_move = None
     for dz in sorted([d for d in range(planes) if d != opposite], key=lambda d: min(d, planes - d)):
-        if back_move is None and min(dz, planes - dz) == max(opposite - 1, 1):
+        if back_move is None and min(dz, planes - dz) == 2:
             back_move = far_product()
         zs = lax.rem(z + planes - dz, planes)
         arrived(dz, PLANE - 1 if dz == 0 else PLANE)

time: 59.7 us -> 59.3 us (level)
  no operation moved by 1% of the time
where the time goes in v6:
time: 59.3 us; the launch traced here: 59.2 us
  Pallas kernels  58.6 us (99%)
  between operations  0.64 us (1%)
    pallas_call x1, Pallas kernels, shards(): pl.pallas_call(functools.partial(kernel, planes, helpers, capacity), out_...  56.9 us
    pallas_call x1, Pallas kernels, shards(): pl.pallas_call(deliver, out_shape=(jax.ShapeDtypeStruct(sketch_shape, F32...  1.63 us

profile of v6, /device:TPU:32, one launch (start us, length us, event | category | flops | bytes accessed | tf_op | source)
XLA Modules:
  0.0 59.2 jit_solution(17682933299213171648)
XLA Ops:
  0.6 56.9 %shard_map.77 = (f32[32,1024]{1,0:T(8,128)}, f32[1,32,768]{2,1,0:T(8,128)}) custom-call(s32[2,256]{1,0:T(2,128)} %bitcast.2, s32[2,256]{1,0:T(2,128)} %bitcast.3, bf16[256,768]{1,0:T(8,128)(2,1)} %query_hbm.1, bf16[1024,768]{1,0:T(8,128)(2,1)} %point_hbm.1, s32[1,4096]{1,0:T(1,128)} %cluster_hbm.1, bf16[32,1024]{1,0:T(8,128)(2,1)} %test_hbm.1), custom_call_target="tpu_custom_call" | custom-call | tf_op jit(solution)/shard_map/pallas_call | solution.py:466
  57.6 1.6 %shard_map.78 = (f32[32,1024]{1,0:T(8,128)}, f32[1,32,768]{2,1,0:T(8,128)}) custom-call(f32[32,1024]{1,0:T(8,128)} %get-tuple-element.4.a_ref, f32[1,32,768]{2,1,0:T(8,128)} %get-tuple-element.5.b_ref), custom_call_target="tpu_custom_call" | custom-call | tf_op jit(solution)/shard_map/pallas_call | solution.py:525

commit v7 on v6

--- a/solution.py
+++ b/solution.py
@@ -195,6 +195,13 @@
     for d in near:
         ship(d)
 
+    if opposite >= 2:
+        advance(2)
+        if opposite > 2:
+            for dz in (2, planes - 2):
+                pack(dz)
+                ship(dz)
+
     def exchange(part, landing, sem):
         copies = []
         for j in range(1, helpers):
@@ -234,13 +241,11 @@
     lead_part[...] = dot(spread, point[...], 1, 0).reshape(helpers, rank, width)
     lead_copies = exchange(lead_part, lead_in, lead_sem)
 
-    for far in range(2, opposite + 1):
+    for far in range(3, opposite + 1):
         advance(far)
         if far < opposite:
             for dz in (far, planes - far):
                 pack(dz)
-                if far < opposite - 1 or far == 2:
-                    ship(dz)
 
     def to_opposite(pair, sem):
         c = pltpu.make_async_remote_copy(
@@ -313,7 +318,10 @@
         return to_opposite(far_back, fback_sem)
 
     back_move = None
-    for dz in sorted([d for d in range(planes) if d != opposite], key=lambda d: min(d, planes - d)):
+    waves = sorted([d for d in range(planes) if d != opposite], key=lambda d: min(d, planes - d))
+    for place_in, dz in enumerate(waves):
+        if place_in == len(waves) - 1:
+            acc = acc[:n] + acc[n:]
         if back_move is None and min(dz, planes - dz) == 2:
             back_move = far_product()
         zs = lax.rem(z + planes - dz, planes)
@@ -332,15 +340,18 @@
             [jnp.where(piece == c + 1.0, lifted[c * rank:(c + 1) * rank], 0.0) for c in range(helpers)],
             axis=0,
         )
-        acc = acc + dot(stack_halves(lifted), rowsy, 1, 0)
+        halved = stack_halves(lifted)
+        if place_in < len(waves) - 1:
+            acc = acc + dot(halved, rowsy, 1, 0)
     if back_move is None:
         back_move = far_product()
-    count_move.wait()
-    product = acc[:n] + acc[n:]
     back_copies = []
     for i in range(pieces):
-        back_part[i] = product[:, cut[i]].reshape(helpers, rank, part_width).astype(BACK)
+        latest = dot(halved, rowsy[:, cut[i]], 1, 0)
+        product = acc[:, cut[i]] + latest[:n] + latest[n:]
+        back_part[i] = product.reshape(helpers, rank, part_width).astype(BACK)
         back_copies.append(exchange(back_part.at[i], back_in.at[i], back_sem.at[i]))
+    count_move.wait()
     for c in range(helpers):
         count_part[c:c + 1, :] = far_count[1, c:c + 1, :] + named[c]
     count_copies = []

time: 59.3 us -> 58.5 us (0.987)
  Pallas kernels: 58.6 us -> 57.7 us
    pallas_call x1, Pallas kernels: 56.9 us -> 56.1 us  [shards(): pl.pallas_call(functools.partial(kernel, planes, helpers, capacity), out_...]
where the time goes in v7:
time: 58.5 us; the launch traced here: 58.4 us
  Pallas kernels  57.7 us (99%)
  between operations  0.64 us (1%)
    pallas_call x1, Pallas kernels, shards(): pl.pallas_call(functools.partial(kernel, planes, helpers, capacity), out_...  56.1 us
    pallas_call x1, Pallas kernels, shards(): pl.pallas_call(deliver, out_shape=(jax.ShapeDtypeStruct(sketch_shape, F32...  1.63 us

profile of v7, /device:TPU:32, one launch (start us, length us, event | category | flops | bytes accessed | tf_op | source)
XLA Modules:
  0.0 58.4 jit_solution(8189783720764312420)
XLA Ops:
  0.6 56.1 %shard_map.77 = (f32[32,1024]{1,0:T(8,128)}, f32[1,32,768]{2,1,0:T(8,128)}) custom-call(s32[2,256]{1,0:T(2,128)} %bitcast.2, s32[2,256]{1,0:T(2,128)} %bitcast.3, bf16[256,768]{1,0:T(8,128)(2,1)} %query_hbm.1, bf16[1024,768]{1,0:T(8,128)(2,1)} %point_hbm.1, s32[1,4096]{1,0:T(1,128)} %cluster_hbm.1, bf16[32,1024]{1,0:T(8,128)(2,1)} %test_hbm.1), custom_call_target="tpu_custom_call" | custom-call | tf_op jit(solution)/shard_map/pallas_call | solution.py:477
  56.7 1.6 %shard_map.78 = (f32[32,1024]{1,0:T(8,128)}, f32[1,32,768]{2,1,0:T(8,128)}) custom-call(f32[32,1024]{1,0:T(8,128)} %get-tuple-element.4.a_ref, f32[1,32,768]{2,1,0:T(8,128)} %get-tuple-element.5.b_ref), custom_call_target="tpu_custom_call" | custom-call | tf_op jit(solution)/shard_map/pallas_call | solution.py:536
